TPU v7x, 128 devices: a whole 4x4x4 slice. The times are simulated.
128 devices in a mesh: row: 16 (over x, z), col: 8 (over y, core).
Axes of the slice: x: 4, y: 4, z: 4, core: 2. Of those that a mesh axis runs over, the one named last changes fastest.
Arguments:
- a_blocks: float32 [4096, 6, 4096], P(('row', 'col')), as said below
- columns: int32 [4096, 6], P(('row', 'col')), may hold values from 0 to 4095, as said below
- tentative: float32 [4096, 4096], P(('row', 'col')), may hold values from -0.75 to 0.75
- aggregate: int32 [4096], P(('row', 'col')), may hold values from 0 to 3, as said below
- owner: int32 [512], P(('row', 'col')), may hold values from 0 to 511, as said below
Outputs:
- coarse_op: float32 [512, 20, 4096], P(('row', 'col'))
Inputs may be any that keep to these rules, and one draw needn't show every extreme that they name: Column 0 of block row n is n. Other columns of block row n lie among the block rows of n's device (32 a device, devices in the order of row+col); for the first 8 rows of a device they may also lie among the last 8 rows of the device before it, and for the last 8 rows among the first 8 rows of the device after it, and each such rim row of a device with that neighbour has one. Columns may repeat; repeated blocks add. `aggregate`: every device uses every number from 0 to 3. `owner`: A permutation of the coarse rows. The coarse rows of a device (a // 4) go to positions owned (position // 4) by devices of the same index along row, at most one to each device, so each device owns 4. The diagonal entries of the blocks a_blocks[n, 0] lie between 1.5 and 8.5.
All inputs are finite; a program needn't handle non-finite values.
Results may differ from a plain program's by a relative error of at most 0.0003.
Values sent between devices are 32-bit elements; how exact they have to be, the bound alone decides.
A program may use at most 256 MiB of HBM per device.

v0:
```python
import jax
import jax.numpy as jnp
from jax import lax
from jax.sharding import PartitionSpec as P

B = 64
BC = 64
K = 6
G = 4
R = 32
H = 8


highest = lax.Precision.HIGHEST
relaxation = 2.0 / 3.0


def padded(block, sides, width):
    for axis, dim in sides:
        count = lax.axis_size(axis)
        forward = [(i, i + 1) for i in range(count - 1)]
        backward = [(target, source) for source, target in forward]
        low = lax.ppermute(
            lax.slice_in_dim(block, block.shape[dim] - width, None, axis=dim), axis, forward
        )
        high = lax.ppermute(lax.slice_in_dim(block, 0, width, axis=dim), axis, backward)
        block = jnp.concatenate([low, block, high], axis=dim)
    return block


def from_behind(block, axis, distance):
    devices = range(lax.axis_size(axis))
    route = [(i - distance, i) for i in devices if i - distance in devices]
    return lax.ppermute(block, axis, route)


def prolong_rows(a_rows, col_rows, own_basis, ext_basis, ext_agg, device):
    row_count = col_rows.shape[0]
    local_index = col_rows - device * R + H
    dev_offset = (local_index >= H).astype(jnp.int32) + (local_index >= R + H).astype(jnp.int32)
    labels = (dev_offset * G + jnp.take(ext_agg, local_index)).astype(jnp.int32)
    a_mats = a_rows.reshape(row_count, K, B, B)
    basis_rows = jnp.take(ext_basis, local_index, axis=0).reshape(row_count, K, B, BC)
    applied = jnp.einsum("ikqp,ikpv->ikqv", a_mats, basis_rows, precision=highest)
    diagonal = jnp.diagonal(a_mats[:, 0], axis1=1, axis2=2)
    first_column = (jnp.arange(K) == 0).astype(applied.dtype)
    smooth = (
        first_column[None, :, None, None] * own_basis.reshape(row_count, 1, B, BC)
        - relaxation * applied / diagonal[:, None, :, None]
    )
    return (smooth.reshape(row_count, K, B * BC), labels)


def dense_rows(ext_smooth, ext_labels):
    onehot = (ext_labels[..., None] == jnp.arange(3 * G, dtype=jnp.int32)).astype(ext_smooth.dtype)
    return jnp.einsum("rmc,rmx->rcx", onehot, ext_smooth, precision=highest)


def apply_rows(a_group, index_group, ext_dense):
    count = index_group.shape[0]
    gathered = jnp.take(ext_dense, index_group, axis=0).reshape(count, K, 3 * G, B, BC)
    a_mats = a_group.reshape(count, K, B, B)
    total = jnp.einsum("sqp,scpw->scqw", a_mats[:, 0], gathered[:, 0], precision=highest)
    for stored in range(1, K):
        total = total + jnp.einsum(
            "sqp,scpw->scqw", a_mats[:, stored], gathered[:, stored], precision=highest
        )
    return total


def coarse_part(smooth, labels, applied_rows):
    count = labels.shape[0]
    onehot = (labels[..., None] == jnp.arange(3 * G, dtype=jnp.int32)).astype(smooth.dtype)
    dense = jnp.einsum("ikl,ikqv->ilqv", onehot, smooth.reshape(count, K, B, BC), precision=highest)
    return jnp.einsum("ilqv,icqw->lcvw", dense, applied_rows, precision=highest)


def local(a_blocks, columns, tentative, aggregate, owner):
    device = lax.axis_index(("row", "col"))
    ext_basis, ext_agg = (
        padded(tentative, ((("row", "col"), 0),), H),
        padded(aggregate, ((("row", "col"), 0),), H),
    )
    smooth, labels = prolong_rows(a_blocks, columns, tentative, ext_basis, ext_agg, device)
    ext_smooth, ext_labels = (
        padded(smooth, ((("row", "col"), 0),), H),
        padded(labels, ((("row", "col"), 0),), H),
    )
    position = jnp.arange(R + 2 * H, dtype=jnp.int32)
    label_shift = jnp.where(position < H, -G, jnp.where(position >= R + H, G, 0)).astype(jnp.int32)
    ext_labels = (ext_labels + label_shift[:, None]).astype(jnp.int32)
    ext_dense = dense_rows(ext_smooth, ext_labels)
    local_index = columns - device * R + H
    group_count = R // 8

    def apply_group(pieces):
        return apply_rows(pieces[0], pieces[1], ext_dense)

    applied_rows = lax.map(
        apply_group,
        (a_blocks.reshape(group_count, 8, K, B * B), local_index.reshape(group_count, 8, K)),
    )
    applied_rows = applied_rows.reshape(R, 3 * G, B, BC)
    partial_value = coarse_part(smooth, labels, applied_rows)
    from_lower = from_behind(partial_value[2 * G :], ("row", "col"), 1)
    from_upper = from_behind(partial_value[:G], ("row", "col"), -1)
    rows_full = jnp.pad(partial_value[G : 2 * G], ((0, 0), (G, G), (0, 0), (0, 0)))
    rows_full = rows_full + jnp.pad(from_lower, ((0, 0), (0, 2 * G), (0, 0), (0, 0)))
    rows_full = rows_full + jnp.pad(from_upper, ((0, 0), (2 * G, 0), (0, 0), (0, 0)))
    coarse_rows = rows_full.reshape(G, 5 * G, BC * BC)
    all_rows, all_owners = (
        lax.all_gather(coarse_rows, "col", axis=0, tiled=True),
        lax.all_gather(owner, "col", axis=0, tiled=True),
    )
    wanted = (all_owners[None, :] == device * G + jnp.arange(G, dtype=jnp.int32)[:, None]).astype(
        jnp.float32
    )
    result = jnp.einsum("ga,acx->gcx", wanted, all_rows, precision=highest)
    return result


def solution(mesh):
    placed = (
        P(("row", "col"), None, None),
        P(("row", "col"), None),
        P(("row", "col"), None),
        P(("row", "col")),
        P(("row", "col")),
    )
    return jax.shard_map(
        local, mesh=mesh, in_specs=placed, out_specs=P(("row", "col"), None, None), check_vma=False
    )
```

profile of v0, /device:TPU:1, one launch (start us, length us, event | category | flops | bytes accessed | tf_op | source)
XLA Modules:
  0.0 726.2 jit_solution(1475862194266021653)
XLA Ops:
  7.3 4.6 collective-permute-start
  14.9 3.6 collective-permute-start.4
  20.4 8.4 %copy.51 = f32[32,6,4096]{0,2,1:T(8,128)} copy(f32[32,6,4096]{2,0,1:T(8,128)} %param.7) | data formatting | bytes 6291456 | tf_op args[0]
  28.9 10.5 %copy.52 = f32[32,6,64,64]{3,2,1,0:T(8,128)} copy(f32[32,6,64,64]{0,3,2,1:T(8,128)} %bitcast.153) | data formatting | bytes 6291456 | tf_op jit(solution)/shard_map/reshape | solution.py:42
  39.4 3.2 slice_bitcast_fusion.26
  46.9 3.6 collective-permute-start.2
  55.8 3.3 gather_fusion.2
  59.1 6.1 gather.22
  65.2 6.6 copy.50
  71.8 13.5 %bitcast_subtract_fusion = f32[32,6,64,64]{2,3,1,0:T(8,128)S(1)} fusion(f32[32,64]{1,0:T(8,128)S(1)} %copy.53, f32[32,64,64]{1,2,0:T(8,128)S(1)} %copy.49, f32[6]{0:T(128)S(1)} %compare_convert_fusion, f32[32,6,64,64]{3,2,1,0:T(8,128)} %copy.52, f32[32,6,64,64]{2,3,1,0:T(8,128)} %copy.50, pred[32,6]{1,0:T(8,128)(4,1)S(1)} %get-tuple-element.56), kind=kOutput, calls=%fused_computation.42 | convolution fusion | flops 607911936 | bytes 9969880 | tf_op jit(solution)/shard_map/ikqp,ikpv->ikqv/dot_general | solution.py:44
  89.4 6.6 copy.78
  96.0 8.4 %copy.61 = f32[32,6,64,64]{3,1,2,0:T(8,128)} copy(f32[32,6,64,64]{2,3,1,0:T(8,128)} %copy-done.2) | data formatting | bytes 6291456 | tf_op jit(solution)/shard_map/sub | solution.py:48
  111.0 3.2 collective-permute-start.7
  114.2 7.1 reshape.186
  121.3 14.8 %fusion.30 = f32[32,12,64,64]{3,1,2,0:T(8,128)} fusion(f32[32,6,64,64]{3,1,2,0:T(8,128)} %copy.61, s32[32,6]{1,0:T(8,128)S(1)} %get-tuple-element.55), kind=kOutput, calls=%fused_computation.54 | convolution fusion | flops 113248512 | bytes 9437952 | tf_op jit(solution)/shard_map/ikl,ikqv->ilqv/dot_general | solution.py:74
  138.2 9.8 %fusion.12 = f32[48,12,4096]{2,1,0:T(8,128)} fusion(f32[8,6,4096]{2,1,0:T(8,128)S(1)} %copy.59, f32[32,6,4096]{2,1,0:T(8,128)S(1)} %copy-done.3, f32[8,6,4096]{2,1,0:T(8,128)S(1)} %copy.57, s32[48,6]{1,0:T(8,128)S(1)} %copy.48), kind=kOutput, calls=%fused_computation.36 | convolution fusion | flops 172232064 | bytes 14156928 | tf_op jit(solution)/shard_map/rmc,rmx->rcx/dot_general | solution.py:56
  148.1 386.7 %while.10 = (s32[]{:T(128)}, f32[4,8,12,64,64]{3,4,2,1,0:T(8,128)}, s32[4,8,6]{2,1,0:T(8,128)S(1)}, f32[48,12,4096]{2,1,0:T(8,128)}, f32[4,8,6,4096]{3,1,0,2:T(8,128)}, /*index=5*/s32[]{:T(128)}) while((s32[]{:T(128)}, f32[4,8,12,64,64]{3,4,2,1,0:T(8,128)}, s32[4,8,6]{2,1,0:T(8,128)S(1)}, f32[48,12,4096]{2,1,0:T(8,128)}, ...), condition=%wide.region_1.2_spmd, body=%wide.region_0.1_spmd.sunk | while | flops 1816266240 | bytes 166730816 | solution.py:99
  148.5 12.3 %gather_fusion = f32[48,12,4096]{2,1,0:T(8,128)} fusion(f32[48,12,4096]{2,1,0:T(8,128)} %get-tuple-element.120, s32[1024]{0:T(1024)S(1)} %pad_clamp_fusion.3), kind=kCustom, calls=%fused_computation.clone.1 | custom fusion | bytes 18874560 | tf_op jit(solution)/shard_map/while/body/eval_jaxpr/jit(_take)/gather | solution.py:61
  160.8 16.9 %reshape.196 = f32[8,6,12,64,64]{4,3,2,1,0:T(8,128)} reshape(f32[48,12,4096]{2,1,0:T(8,128)} %gather_fusion) | data formatting | bytes 18874368 | tf_op jit(solution)/shard_map/while/body/eval_jaxpr/jit(_take)/gather | solution.py:61
  177.7 18.7 %copy.103 = f32[8,6,12,64,64]{3,4,2,0,1:T(8,128)} copy(f32[8,6,12,64,64]{4,3,2,1,0:T(8,128)} %reshape.196) | data formatting | bytes 18874368 | tf_op jit(solution)/shard_map/while/body/eval_jaxpr/jit(_take)/gather | solution.py:61
  196.5 13.8 %broadcast_select_fusion.2 = f32[8,6,12,64,64]{3,4,2,0,1:T(8,128)} fusion(f32[8,6,12,64,64]{3,4,2,0,1:T(8,128)} %copy.103, pred[8,6]{0,1:T(8,128)(4,1)S(1)} %copy.104), kind=kLoop, calls=%fused_computation.4.clone.1 | loop fusion | flops 2359296 | bytes 18874416 | tf_op jit(solution)/shard_map/while/body/eval_jaxpr/jit(_take)/select_n | solution.py:61
  212.1 5.6 fusion.53
  217.7 5.7 fusion.54
  223.5 5.0 fusion.55
  228.5 4.0 fusion.56
  232.5 5.4 fusion.52
  237.9 6.8 bitcast_dynamic-update-slice_fusion.2
  245.0 12.3 %gather_fusion = f32[48,12,4096]{2,1,0:T(8,128)} fusion(f32[48,12,4096]{2,1,0:T(8,128)} %get-tuple-element.120, s32[1024]{0:T(1024)S(1)} %pad_clamp_fusion.3), kind=kCustom, calls=%fused_computation.clone.1 | custom fusion | bytes 18874560 | tf_op jit(solution)/shard_map/while/body/eval_jaxpr/jit(_take)/gather | solution.py:61
  257.3 16.9 %reshape.196 = f32[8,6,12,64,64]{4,3,2,1,0:T(8,128)} reshape(f32[48,12,4096]{2,1,0:T(8,128)} %gather_fusion) | data formatting | bytes 18874368 | tf_op jit(solution)/shard_map/while/body/eval_jaxpr/jit(_take)/gather | solution.py:61
  274.2 18.7 %copy.103 = f32[8,6,12,64,64]{3,4,2,0,1:T(8,128)} copy(f32[8,6,12,64,64]{4,3,2,1,0:T(8,128)} %reshape.196) | data formatting | bytes 18874368 | tf_op jit(solution)/shard_map/while/body/eval_jaxpr/jit(_take)/gather | solution.py:61
  293.0 13.8 %broadcast_select_fusion.2 = f32[8,6,12,64,64]{3,4,2,0,1:T(8,128)} fusion(f32[8,6,12,64,64]{3,4,2,0,1:T(8,128)} %copy.103, pred[8,6]{0,1:T(8,128)(4,1)S(1)} %copy.104), kind=kLoop, calls=%fused_computation.4.clone.1 | loop fusion | flops 2359296 | bytes 18874416 | tf_op jit(solution)/shard_map/while/body/eval_jaxpr/jit(_take)/select_n | solution.py:61
  308.6 5.6 fusion.53
  314.2 5.7 fusion.54
  320.0 5.0 fusion.55
  325.0 4.0 fusion.56
  329.0 5.4 fusion.52
  334.5 6.8 bitcast_dynamic-update-slice_fusion.2
  341.5 12.3 %gather_fusion = f32[48,12,4096]{2,1,0:T(8,128)} fusion(f32[48,12,4096]{2,1,0:T(8,128)} %get-tuple-element.120, s32[1024]{0:T(1024)S(1)} %pad_clamp_fusion.3), kind=kCustom, calls=%fused_computation.clone.1 | custom fusion | bytes 18874560 | tf_op jit(solution)/shard_map/while/body/eval_jaxpr/jit(_take)/gather | solution.py:61
  353.8 16.9 %reshape.196 = f32[8,6,12,64,64]{4,3,2,1,0:T(8,128)} reshape(f32[48,12,4096]{2,1,0:T(8,128)} %gather_fusion) | data formatting | bytes 18874368 | tf_op jit(solution)/shard_map/while/body/eval_jaxpr/jit(_take)/gather | solution.py:61
  370.7 18.7 %copy.103 = f32[8,6,12,64,64]{3,4,2,0,1:T(8,128)} copy(f32[8,6,12,64,64]{4,3,2,1,0:T(8,128)} %reshape.196) | data formatting | bytes 18874368 | tf_op jit(solution)/shard_map/while/body/eval_jaxpr/jit(_take)/gather | solution.py:61
  389.5 13.8 %broadcast_select_fusion.2 = f32[8,6,12,64,64]{3,4,2,0,1:T(8,128)} fusion(f32[8,6,12,64,64]{3,4,2,0,1:T(8,128)} %copy.103, pred[8,6]{0,1:T(8,128)(4,1)S(1)} %copy.104), kind=kLoop, calls=%fused_computation.4.clone.1 | loop fusion | flops 2359296 | bytes 18874416 | tf_op jit(solution)/shard_map/while/body/eval_jaxpr/jit(_take)/select_n | solution.py:61
  405.1 5.6 fusion.53
  410.7 5.7 fusion.54
  416.5 5.0 fusion.55
  421.5 4.0 fusion.56
  425.6 5.4 fusion.52
  431.0 6.9 bitcast_dynamic-update-slice_fusion.2
  438.1 12.3 %gather_fusion = f32[48,12,4096]{2,1,0:T(8,128)} fusion(f32[48,12,4096]{2,1,0:T(8,128)} %get-tuple-element.120, s32[1024]{0:T(1024)S(1)} %pad_clamp_fusion.3), kind=kCustom, calls=%fused_computation.clone.1 | custom fusion | bytes 18874560 | tf_op jit(solution)/shard_map/while/body/eval_jaxpr/jit(_take)/gather | solution.py:61
  450.4 16.9 %reshape.196 = f32[8,6,12,64,64]{4,3,2,1,0:T(8,128)} reshape(f32[48,12,4096]{2,1,0:T(8,128)} %gather_fusion) | data formatting | bytes 18874368 | tf_op jit(solution)/shard_map/while/body/eval_jaxpr/jit(_take)/gather | solution.py:61
  467.3 18.7 %copy.103 = f32[8,6,12,64,64]{3,4,2,0,1:T(8,128)} copy(f32[8,6,12,64,64]{4,3,2,1,0:T(8,128)} %reshape.196) | data formatting | bytes 18874368 | tf_op jit(solution)/shard_map/while/body/eval_jaxpr/jit(_take)/gather | solution.py:61
  486.1 13.8 %broadcast_select_fusion.2 = f32[8,6,12,64,64]{3,4,2,0,1:T(8,128)} fusion(f32[8,6,12,64,64]{3,4,2,0,1:T(8,128)} %copy.103, pred[8,6]{0,1:T(8,128)(4,1)S(1)} %copy.104), kind=kLoop, calls=%fused_computation.4.clone.1 | loop fusion | flops 2359296 | bytes 18874416 | tf_op jit(solution)/shard_map/while/body/eval_jaxpr/jit(_take)/select_n | solution.py:61
  501.7 5.6 fusion.53
  507.3 5.7 fusion.54
  513.1 5.0 fusion.55
  518.1 4.0 fusion.56
  522.1 5.4 fusion.52
  527.6 6.8 bitcast_dynamic-update-slice_fusion.2
  534.8 50.4 %fusion.22 = f32[12,12,64,64]{2,3,0,1:T(8,128)S(1)} fusion(f32[32,12,64,64]{3,1,2,0:T(8,128)} %fusion.30, f32[32,12,64,64,1]{2,3,1,0,4:T(8,128)} %bitcast.157), kind=kOutput, calls=%fused_computation.48 | convolution fusion | flops 14495514624 | bytes 14942208 | tf_op jit(solution)/shard_map/ilqv,icqw->lcvw/dot_general | solution.py:75
  590.3 15.2 %collective-permute-done.8 = f32[4,12,64,64]{2,3,0,1:T(8,128)S(1)} collective-permute-done((f32[4,12,64,64]{2,3,0,1:T(8,128)S(1)}, f32[4,12,64,64]{2,3,0,1:T(8,128)S(1)}, u32[]{:S(2)}, u32[]{:S(2)}) %collective-permute-start.8) | collective-permute-done | bytes 786464 | tf_op jit(solution)/shard_map/ppermute | solution.py:34
  605.5 4.4 collective-permute-done.9
  612.6 3.1 reshape.187
  617.2 18.5 %all-reduce.3 = s32[32]{0:T(128)S(1)} all-reduce(s32[32]{0:T(128)S(1)} %dynamic-update-slice), channel_id=1, replica_groups=mesh['row'=16,'col'=8] {'col'}, use_global_device_ids=true, to_apply=%add.3 | all-reduce | flops 32 | bytes 256
  635.7 68.9 %all-gather.2.cloned.1.call-done = f32[32,20,4096]{2,1,0:T(8,128)} async-done(((f32[4,20,4096]{2,1,0:T(8,128)}), f32[32,20,4096]{2,1,0:T(8,128)}) %all-gather.2.cloned.1.call-update) | async-done | bytes 10485776 | tf_op jit(solution)/shard_map/all_gather | solution.py:112
  704.6 14.5 %fusion.10 = f32[4,20,4096]{2,0,1:T(4,128)} fusion(f32[32,20,4096]{2,1,0:T(8,128)} %all-gather.2.cloned.1.call-done, s32[32]{0:T(128)S(1)} %all-reduce.3, s32[4]{0:T(128)S(1)} %iota_add_fusion), kind=kOutput, calls=%fused_computation.34 | convolution fusion | flops 125829248 | bytes 11796624 | tf_op jit(solution)/shard_map/ga,acx->gcx/dot_general | solution.py:118
  (121 shorter events, 45.3 us)
Async XLA Ops:
  6.5 698.1 %all-gather.2.cloned.1.call-start = ((), (), s32[]{:S(2)}) async-start(), calls=%async_computation | async-start | bytes 14155776 | tf_op jit(solution)/shard_map/all_gather | solution.py:112
  7.3 37.8 %collective-permute-start = (s32[8]{0:T(128)S(1)}, s32[8]{0:T(128)S(1)}, u32[]{:S(2)}, u32[]{:S(2)}) collective-permute-start(s32[8]{0:T(128)S(1)} %get-tuple-element.68), channel_id=1, source_target_pairs={{0,1},{1,2},{2,3},{3,4},{4,5},{5,6},{6,7},{7,8},{8,9},{9,10},{10,1... | collective-permute-start | bytes 104 | tf_op jit(solution)/shard_map/ppermute | solution.py:23
  11.9 33.2 %collective-permute-start.1 = (s32[8]{0:T(128)S(1)}, s32[8]{0:T(128)S(1)}, u32[]{:S(2)}, u32[]{:S(2)}) collective-permute-start(s32[8]{0:T(128)S(1)} %get-tuple-element.69), channel_id=1, source_target_pairs={{1,0},{2,1},{3,2},{4,3},{5,4},{6,5},{7,6},{8,7},{9,8},{10,9},{11,1... | collective-permute-start | bytes 104 | tf_op jit(solution)/shard_map/ppermute | solution.py:26
  14.9 40.9 %collective-permute-start.4 = (f32[8,4096]{1,0:T(8,128)S(1)}, f32[8,4096]{1,0:T(8,128)S(1)}, u32[]{:S(2)}, u32[]{:S(2)}) collective-permute-start(f32[8,4096]{1,0:T(8,128)S(1)} %get-tuple-element.62), channel_id=1, source_target_pairs={{0,1},{1,2},{2,3},{3,4},{4,5},{5,6},{6,7},{7,8},{8,9},{9,10},{10,1... | collective-permute-start | bytes 393224 | tf_op jit(solution)/shard_map/ppermute | solution.py:23
  18.5 37.3 %collective-permute-start.5 = (f32[8,4096]{1,0:T(8,128)S(1)}, f32[8,4096]{1,0:T(8,128)S(1)}, u32[]{:S(2)}, u32[]{:S(2)}) collective-permute-start(f32[8,4096]{1,0:T(8,128)S(1)} %get-tuple-element.63), channel_id=1, source_target_pairs={{1,0},{2,1},{3,2},{4,3},{5,4},{6,5},{7,6},{8,7},{9,8},{10,9},{11,1... | collective-permute-start | bytes 393224 | tf_op jit(solution)/shard_map/ppermute | solution.py:26
  28.9 13.7 %copy-start.4 = (f32[32,4096]{1,0:T(8,128)S(1)}, f32[32,4096]{1,0:T(8,128)}, u32[]{:S(2)}) copy-start(f32[32,4096]{1,0:T(8,128)} %param.9) | copy-start | bytes 1572868
  39.4 3.6 copy-start.6
  39.4 5.8 copy-start.5
  46.9 5.7 collective-permute-start.2
  50.6 4.9 collective-permute-start.3
  85.3 2.6 copy-start.2
  107.6 28.5 %collective-permute-start.6 = (f32[8,6,4096]{2,0,1:T(8,128)}, f32[8,6,4096]{2,0,1:T(8,128)}, u32[]{:S(2)}, u32[]{:S(2)}) collective-permute-start(f32[8,6,4096]{2,0,1:T(8,128)} %slice.86), channel_id=1, source_target_pairs={{0,1},{1,2},{2,3},{3,4},{4,5},{5,6},{6,7},{7,8},{8,9},{9,10},{10,1... | collective-permute-start | bytes 2359304 | tf_op jit(solution)/shard_map/ppermute | solution.py:23
  111.0 26.7 %collective-permute-start.7 = (f32[8,6,4096]{2,0,1:T(8,128)S(1)}, f32[8,6,4096]{2,0,1:T(8,128)S(1)}, u32[]{:S(2)}, u32[]{:S(2)}) collective-permute-start(f32[8,6,4096]{2,0,1:T(8,128)S(1)} %slice.88), channel_id=1, source_target_pairs={{1,0},{2,1},{3,2},{4,3},{5,4},{6,5},{7,6},{8,7},{9,8},{10,9},{11,1... | collective-permute-start | bytes 2359304 | tf_op jit(solution)/shard_map/ppermute | solution.py:26
  121.3 16.9 %copy-start.3 = (f32[32,6,4096]{2,1,0:T(8,128)S(1)}, f32[32,6,4096]{2,1,0:T(8,128)}, u32[]{:S(2)}) copy-start(f32[32,6,4096]{2,1,0:T(8,128)} %reshape.186) | copy-start | bytes 9437188
  212.1 11.4 %copy-start.1 = (f32[8,6,64,64]{3,2,0,1:T(8,128)}, f32[8,6,64,64]{3,2,0,1:T(8,128)S(1)}, u32[]{:S(2)}) copy-start(f32[8,6,64,64]{3,2,0,1:T(8,128)S(1)} %reshape.197) | copy-start | bytes 2359300 | tf_op jit(solution)/shard_map/while
  212.1 16.4 %copy-start = (f32[8,6,12,64,64]{3,4,2,0,1:T(8,128)S(1)}, f32[8,6,12,64,64]{3,4,2,0,1:T(8,128)}, u32[]{:S(2)}) copy-start(f32[8,6,12,64,64]{3,4,2,0,1:T(8,128)} %broadcast_select_fusion.2) | copy-start | bytes 28311556 | tf_op jit(solution)/shard_map/while
  308.6 11.4 %copy-start.1 = (f32[8,6,64,64]{3,2,0,1:T(8,128)}, f32[8,6,64,64]{3,2,0,1:T(8,128)S(1)}, u32[]{:S(2)}) copy-start(f32[8,6,64,64]{3,2,0,1:T(8,128)S(1)} %reshape.197) | copy-start | bytes 2359300 | tf_op jit(solution)/shard_map/while
  308.6 16.4 %copy-start = (f32[8,6,12,64,64]{3,4,2,0,1:T(8,128)S(1)}, f32[8,6,12,64,64]{3,4,2,0,1:T(8,128)}, u32[]{:S(2)}) copy-start(f32[8,6,12,64,64]{3,4,2,0,1:T(8,128)} %broadcast_select_fusion.2) | copy-start | bytes 28311556 | tf_op jit(solution)/shard_map/while
  405.1 11.4 %copy-start.1 = (f32[8,6,64,64]{3,2,0,1:T(8,128)}, f32[8,6,64,64]{3,2,0,1:T(8,128)S(1)}, u32[]{:S(2)}) copy-start(f32[8,6,64,64]{3,2,0,1:T(8,128)S(1)} %reshape.197) | copy-start | bytes 2359300 | tf_op jit(solution)/shard_map/while
  405.1 16.4 %copy-start = (f32[8,6,12,64,64]{3,4,2,0,1:T(8,128)S(1)}, f32[8,6,12,64,64]{3,4,2,0,1:T(8,128)}, u32[]{:S(2)}) copy-start(f32[8,6,12,64,64]{3,4,2,0,1:T(8,128)} %broadcast_select_fusion.2) | copy-start | bytes 28311556 | tf_op jit(solution)/shard_map/while
  501.7 11.4 %copy-start.1 = (f32[8,6,64,64]{3,2,0,1:T(8,128)}, f32[8,6,64,64]{3,2,0,1:T(8,128)S(1)}, u32[]{:S(2)}) copy-start(f32[8,6,64,64]{3,2,0,1:T(8,128)S(1)} %reshape.197) | copy-start | bytes 2359300 | tf_op jit(solution)/shard_map/while
  501.7 16.4 %copy-start = (f32[8,6,12,64,64]{3,4,2,0,1:T(8,128)S(1)}, f32[8,6,12,64,64]{3,4,2,0,1:T(8,128)}, u32[]{:S(2)}) copy-start(f32[8,6,12,64,64]{3,4,2,0,1:T(8,128)} %broadcast_select_fusion.2) | copy-start | bytes 28311556 | tf_op jit(solution)/shard_map/while
  585.9 19.6 %collective-permute-start.8 = (f32[4,12,64,64]{2,3,0,1:T(8,128)S(1)}, f32[4,12,64,64]{2,3,0,1:T(8,128)S(1)}, u32[]{:S(2)}, u32[]{:S(2)}) collective-permute-start(f32[4,12,64,64]{2,3,0,1:T(8,128)S(1)} %get-tuple-element.61), channel_id=1, source_target_pairs={{0,1},{1,2},{2,3},{3,4},{4,5},{5,6},{6,7},{7,8},{8,9},{9,10},{10,1... | collective-permute-start | bytes 2359304 | tf_op jit(solution)/shard_map/ppermute | solution.py:34
  588.2 21.7 %collective-permute-start.9 = (f32[4,12,64,64]{2,3,0,1:T(8,128)S(1)}, f32[4,12,64,64]{2,3,0,1:T(8,128)S(1)}, u32[]{:S(2)}, u32[]{:S(2)}) collective-permute-start(f32[4,12,64,64]{2,3,0,1:T(8,128)S(1)} %get-tuple-element.60), channel_id=1, source_target_pairs={{1,0},{2,1},{3,2},{4,3},{5,4},{6,5},{7,6},{8,7},{9,8},{10,9},{11,1... | collective-permute-start | bytes 2359304 | tf_op jit(solution)/shard_map/ppermute | solution.py:34
  610.5 5.3 copy-start.8
  610.5 6.5 copy-start.7
Sparse Core Ops, SparseCore 0:
  615.8 88.7 all-gather.1
where the time goes:
time: 739 us; the launch traced here: 726 us
  local copies, waits for them, and re-layouts  284 us (38%)
  matrix products  233 us (32%)
  waiting for transfers between devices  91.4 us (12%)
  other arithmetic  56.1 us (8%)
  starting transfers between devices  27.7 us (4%)
  blocking collectives  18.5 us (3%)
  between operations  14.6 us (2%)
    gather x12, local copies, waits for them, and re-layouts, apply_rows(): jnp.take(ext_dense, index_group, axis=0).reshape(count, K, 3 * G, B, BC)  192 us
    dot_general x20, matrix products, apply_rows(): jnp.einsum('sqp,scpw->scqw', a_mats[:, stored], gathered[:, stored], prec...  103 us
    all_gather x1, waiting for transfers between devices, local(): lax.all_gather(coarse_rows, 'col', axis=0, tiled=True)  68.9 us
    select_n x8, other arithmetic, apply_rows(): jnp.take(ext_dense, index_group, axis=0).reshape(count, K, 3 * G, B, BC)  55.2 us
    dot_general x1, matrix products, coarse_part(): return jnp.einsum('ilqv,icqw->lcvw', dense, applied_rows, precision=highest)  50.4 us
    dot_general x4, matrix products, apply_rows(): jnp.einsum('sqp,scpw->scqw', a_mats[:, 0], gathered[:, 0], precision=high...  27.3 us
    ppermute x2, waiting for transfers between devices, from_behind(): return lax.ppermute(block, axis, route)  19.6 us
    unnamed x1, blocking collectives  18.5 us
  transfers between devices with their start and end apart: 11, of which 4 were waited for; matrix products, arithmetic and copies ran while one was open for 7% of the time, Pallas kernels for 0%

commit v1 on v0

v1 whole, which is shorter than its diff:
```python
import functools

import jax
import jax.numpy as jnp
from jax import lax
from jax.experimental import pallas as pl
from jax.experimental.pallas import tpu as pltpu
from jax.sharding import PartitionSpec as P

B = 64
K = 6
G = 4
R = 32
H = 8
BB = B * B
GW = G * B
LANES = 128
relaxation = 2.0 / 3.0
f32 = jnp.float32
bf16 = jnp.bfloat16


def lane_low(rows):
    return lax.broadcasted_iota(jnp.int32, (rows, LANES), 1) < B


def natural_dup(half_rows, scratch):
    low = lane_low(B // 2)
    swapped = pltpu.roll(half_rows, B, 1)
    scratch[pl.ds(0, B // 2, stride=2), :] = jnp.where(low, half_rows, swapped)
    scratch[pl.ds(1, B // 2, stride=2), :] = jnp.where(low, swapped, half_rows)


def smooth_kernel(cols, aggs, a_ref, t_low, t_own, t_high, p_ref, aa_ref, flat, nat, t_nat, t_split):
    step = pl.program_id(0)
    rows = a_ref.shape[0]
    low = lane_low(B)

    @pl.when(step == 0)
    def _():
        for chunk in range(R // 8 + 2):
            source = t_low if chunk == 0 else t_high if chunk == R // 8 + 1 else t_own
            first = 0 if chunk in (0, R // 8 + 1) else (chunk - 1) * 8
            for c in range(B // 2):
                flat[pl.ds(c * 8, 8), :] = source[first : first + 8, c * LANES : (c + 1) * LANES]

            def one(j, carry):
                n = chunk * 8 + j
                natural_dup(flat[pl.ds(j, B // 2, stride=8), :], t_nat.at[n])
                value = t_nat[n]
                high = value.astype(bf16)
                t_split[n, 0:B, :] = high
                t_split[n, B : 2 * B, :] = (value - high.astype(f32)).astype(bf16)
                return carry

            lax.fori_loop(0, 8, one, 0)

    sub = lax.broadcasted_iota(jnp.int32, (B, LANES), 0)
    lane = lax.broadcasted_iota(jnp.int32, (B, LANES), 1)
    on_diagonal = sub == lane

    for r in range(rows):
        n = step * rows + r
        for c in range(B // 2):
            flat[pl.ds(c * 8, K), :] = a_ref[r, :, c * LANES : (c + 1) * LANES]
        for part in range(4):
            p_ref[r, :, part * LANES : (part + 1) * LANES] = jnp.zeros((B, LANES), f32)
        scale = None
        for k in range(K):
            ci = cols[n * K + k]
            natural_dup(flat[pl.ds(k, B // 2, stride=8), :], nat.at[k % 2])
            value = nat[k % 2]
            if k == 0:
                diagonal = jnp.sum(jnp.where(on_diagonal, value, 0.0), axis=1, keepdims=True)
                scale = relaxation / diagonal
            high = value.astype(bf16).astype(f32)
            pieces = jnp.where(low, high, value - high).astype(bf16)
            aa_ref[r, k] = pieces
            basis = t_split[ci]
            weights = jnp.concatenate([basis[:B], basis[:B], basis[B:], basis[B:]], axis=0)
            applied = jnp.dot(
                jnp.concatenate([pieces, pieces], axis=1), weights, preferred_element_type=f32
            )
            smooth = -applied * scale
            if k == 0:
                smooth = smooth + t_nat[n + H]
            label = aggs[ci]
            outside = jnp.logical_or(ci < H, ci >= R + H).astype(jnp.int32)
            place = pl.multiple_of((outside * 2 + label // 2) * LANES, LANES)
            keep = jnp.where(low, 1 - label % 2, label % 2) == 1
            window = (r, slice(None), pl.ds(place, LANES))
            p_ref[window] = p_ref[window] + jnp.where(keep, smooth, 0.0)


def smooth_rows(a_blocks, t_low, t_own, t_high, cols, aggs):
    rows = 4
    whole = lambda shape: pl.BlockSpec(shape, lambda i, *_: (0,) * len(shape))
    return pl.pallas_call(
        smooth_kernel,
        out_shape=(
            jax.ShapeDtypeStruct((R, B, 2 * GW), f32),
            jax.ShapeDtypeStruct((R, K, B, LANES), bf16),
        ),
        grid_spec=pltpu.PrefetchScalarGridSpec(
            num_scalar_prefetch=2,
            grid=(R // rows,),
            in_specs=[
                pl.BlockSpec((rows, K, BB), lambda i, *_: (i, 0, 0)),
                whole((H, BB)),
                whole((R, BB)),
                whole((H, BB)),
            ],
            out_specs=(
                pl.BlockSpec((rows, B, 2 * GW), lambda i, *_: (i, 0, 0)),
                pl.BlockSpec((rows, K, B, LANES), lambda i, *_: (i, 0, 0, 0)),
            ),
            scratch_shapes=[
                pltpu.VMEM((B // 2 * 8, LANES), f32),
                pltpu.VMEM((2, B, LANES), f32),
                pltpu.VMEM((R + 2 * H, B, LANES), f32),
                pltpu.VMEM((R + 2 * H, 2 * B, LANES), bf16),
            ],
        ),
        compiler_params=pltpu.CompilerParams(vmem_limit_bytes=40 << 20),
        name="smooth",
    )(cols, aggs, a_blocks, t_low, t_own, t_high)


def coarse_kernel(cols, aa_ref, p_own, p_low, p_high, out_ref, p_split, ap):
    step = pl.program_id(0)
    rows = aa_ref.shape[0]

    def split(value):
        high = value.astype(bf16)
        return high, (value - high.astype(f32)).astype(bf16)

    @pl.when(step == 0)
    def _():
        out_ref[...] = jnp.zeros_like(out_ref)

        def own(n, carry):
            high, low = split(p_own[n])
            p_split[n + H, 0:B, :] = high
            p_split[n + H, B : 2 * B, :] = low
            return carry

        lax.fori_loop(0, R, own, 0)
        for source, base in ((p_low, 0), (p_high, R + H)):

            def halo(n, carry, source=source, base=base):
                for half in range(2):
                    high, low = split(source[n, :, (1 - half) * GW : (2 - half) * GW])
                    p_split[base + n, 0:B, half * GW : (half + 1) * GW] = high
                    p_split[base + n, B : 2 * B, half * GW : (half + 1) * GW] = low
                return carry

            lax.fori_loop(0, H, halo, 0)

    ap[0] = jnp.zeros_like(ap[0])
    ap[2] = jnp.zeros_like(ap[2])
    for r in range(rows):
        n = step * rows + r
        total = jnp.zeros((B, GW), f32)
        for k in range(K):
            ci = cols[n * K + k]
            pieces = aa_ref[r, k]
            basis = p_split[ci]
            weights = jnp.concatenate([basis[:B], basis[:B], basis[B:], basis[B:]], axis=0)
            applied = jnp.dot(
                jnp.concatenate([pieces, pieces], axis=1), weights, preferred_element_type=f32
            )
            total = total + applied[:, :GW]
            window = (jnp.where(ci < R // 2, 0, 2), slice(r * B, (r + 1) * B), slice(None))
            ap[window] = ap[window] + applied[:, GW:]
        ap[1, r * B : (r + 1) * B, :] = total

    def product(left, right):
        return lax.dot_general(left, right, (((0,), (0,)), ((), ())), preferred_element_type=f32)

    base = step * rows + H
    p_all = p_split[pl.ds(base, rows)]
    p_high_part = p_all[:, :B, :].reshape(rows * B, 2 * GW)
    p_low_part = p_all[:, B:, :].reshape(rows * B, 2 * GW)
    ap_split = [split(ap[g]) for g in range(3)]

    def add(target, lanes):
        for g in range(3):
            high, low = ap_split[g]
            value = product(p_high_part[:, lanes], high)
            value = value + product(p_low_part[:, lanes], high)
            value = value + product(p_high_part[:, lanes], low)
            for half in range(2):
                out_ref[target, 2 * g + half] += value[:, half * LANES : (half + 1) * LANES]

    add(1, slice(0, GW))

    @pl.when(step < H // rows)
    def _():
        add(0, slice(GW, 2 * GW))

    @pl.when(step >= (R - H) // rows)
    def _():
        add(2, slice(GW, 2 * GW))


def coarse_parts(pieces, p_own, p_low, p_high, cols):
    rows = 4
    whole = lambda shape: pl.BlockSpec(shape, lambda i, *_: (0,) * len(shape))
    return pl.pallas_call(
        coarse_kernel,
        out_shape=jax.ShapeDtypeStruct((3, 6, GW, LANES), f32),
        grid_spec=pltpu.PrefetchScalarGridSpec(
            num_scalar_prefetch=1,
            grid=(R // rows,),
            in_specs=[
                pl.BlockSpec((rows, K, B, LANES), lambda i, *_: (i, 0, 0, 0)),
                whole((R, B, 2 * GW)),
                whole((H, B, 2 * GW)),
                whole((H, B, 2 * GW)),
            ],
            out_specs=whole((3, 6, GW, LANES)),
            scratch_shapes=[
                pltpu.VMEM((R + 2 * H, 2 * B, 2 * GW), bf16),
                pltpu.VMEM((3, rows * B, GW), f32),
            ],
        ),
        compiler_params=pltpu.CompilerParams(vmem_limit_bytes=48 << 20),
        name="coarse",
    )(cols, pieces, p_own, p_low, p_high)


def assemble_kernel(pick, own, lower, upper, out_ref):
    for j in range(10):
        terms = []
        if j < 6:
            terms.append(lower[j])
        if 2 <= j < 8:
            terms.append(own[j - 2])
        if j >= 4:
            terms.append(upper[j - 4])
        out_ref[0, j] = functools.reduce(jnp.add, terms)


def assemble(own, lower, upper, pick, slots):
    spec = pl.BlockSpec((6, B, LANES), lambda j, pick: (0, pick[j], 0))
    return pl.pallas_call(
        assemble_kernel,
        out_shape=jax.ShapeDtypeStruct((slots, 10, B, LANES), f32),
        grid_spec=pltpu.PrefetchScalarGridSpec(
            num_scalar_prefetch=1,
            grid=(slots,),
            in_specs=[spec, spec, spec],
            out_specs=pl.BlockSpec((1, 10, B, LANES), lambda j, pick: (j, 0, 0, 0)),
        ),
        name="assemble",
    )(pick, own, lower, upper)


def exchange_kernel(slots, send, codes, recv, got, send_sem, recv_sem, code_send, code_recv, own_sem):
    me = lax.axis_index("col")
    row = lax.axis_index("row")
    barrier = pltpu.get_barrier_semaphore()
    for s in range(1, slots):
        peer = lax.rem(me + s, slots)
        pl.semaphore_signal(
            barrier, inc=1, device_id=(row, peer), device_id_type=pl.DeviceIdType.MESH
        )
    pl.semaphore_wait(barrier, slots - 1)
    copies = []
    for s in range(1, slots):
        peer = lax.rem(me + s, slots)
        for source, target, here, there in (
            (codes, got, code_send, code_recv),
            (send, recv, send_sem, recv_sem),
        ):
            copy = pltpu.make_async_remote_copy(
                src_ref=source.at[peer],
                dst_ref=target.at[me],
                send_sem=here.at[s],
                recv_sem=there.at[s],
                device_id=(row, peer),
                device_id_type=pl.DeviceIdType.MESH,
            )
            copy.start()
            copies.append(copy)
    for index, (source, target) in enumerate(((codes, got), (send, recv))):
        copy = pltpu.make_async_copy(source.at[me], target.at[me], own_sem.at[index])
        copy.start()
        copies.append(copy)
    for copy in copies:
        copy.wait()


def exchange(send, codes, slots):
    anywhere = pl.BlockSpec(memory_space=pl.ANY)
    dma = pltpu.SemaphoreType.DMA
    return pl.pallas_call(
        functools.partial(exchange_kernel, slots),
        out_shape=(
            jax.ShapeDtypeStruct(send.shape, send.dtype),
            jax.ShapeDtypeStruct(codes.shape, codes.dtype),
        ),
        in_specs=[anywhere, anywhere],
        out_specs=(anywhere, anywhere),
        scratch_shapes=[dma((slots,)), dma((slots,)), dma((slots,)), dma((slots,)), dma((2,))],
        compiler_params=pltpu.CompilerParams(collective_id=0, has_side_effects=True),
        name="exchange",
    )(send, codes)


def final_kernel(source, in_ref, out_ref, pairs):
    low = lane_low(B // 2)
    for j in range(5 * G // 2):
        even = in_ref[0, j, pl.ds(0, B // 2, stride=2), :]
        odd = in_ref[0, j, pl.ds(1, B // 2, stride=2), :]
        pairs[pl.ds(2 * j * (B // 2), B // 2), :] = jnp.where(low, even, pltpu.roll(odd, B, 1))
        pairs[pl.ds((2 * j + 1) * (B // 2), B // 2), :] = jnp.where(low, pltpu.roll(even, B, 1), odd)
    for c in range(B // 2):
        out_ref[0, :, c * LANES : (c + 1) * LANES] = pairs[pl.ds(c, 5 * G, stride=B // 2), :]


def final(recv, source):
    return pl.pallas_call(
        final_kernel,
        out_shape=jax.ShapeDtypeStruct((G, 5 * G, BB), f32),
        grid_spec=pltpu.PrefetchScalarGridSpec(
            num_scalar_prefetch=1,
            grid=(G,),
            in_specs=[pl.BlockSpec((1, 10, B, LANES), lambda g, source: (source[g], 0, 0, 0))],
            out_specs=pl.BlockSpec((1, 5 * G, BB), lambda g, source: (g, 0, 0)),
            scratch_shapes=[pltpu.VMEM((5 * G * B // 2, LANES), f32)],
        ),
        name="final",
    )(source, recv)


def shift(value, distance):
    axes = ("row", "col")
    count = lax.axis_size(axes)
    route = [(i, i + distance) for i in range(count) if 0 <= i + distance < count]
    return lax.ppermute(value, axes, route)


def local(a_blocks, columns, tentative, aggregate, owner):
    axes = ("row", "col")
    device = lax.axis_index(axes)
    slots = lax.axis_size("col")
    t_low, t_high = shift(tentative[R - H :], 1), shift(tentative[:H], -1)
    aggs = jnp.concatenate([shift(aggregate[R - H :], 1), aggregate, shift(aggregate[:H], -1)])
    cols = (columns - device * R + H).reshape(-1)
    p_own, pieces = smooth_rows(a_blocks, t_low, tentative, t_high, cols, aggs)
    p_low, p_high = shift(p_own[R - H :], 1), shift(p_own[:H], -1)
    parts = coarse_parts(pieces, p_own, p_low, p_high, cols)
    from_lower, from_upper = shift(parts[2], 1), shift(parts[0], -1)

    target = (owner // G) % slots
    hits = target[None, :] == jnp.arange(slots, dtype=jnp.int32)[:, None]
    pick = jnp.sum(hits * jnp.arange(G, dtype=jnp.int32)[None, :], axis=1).astype(jnp.int32)
    place = jnp.sum(hits * (owner % G + 1)[None, :], axis=1).astype(jnp.int32)
    codes = jnp.broadcast_to(place[:, None, None], (slots, 8, LANES))
    send = assemble(parts[1], from_lower, from_upper, pick, slots)
    recv, got = exchange(send, codes, slots)
    places = got[:, 0, 0]
    wanted = places[None, :] == jnp.arange(1, G + 1, dtype=jnp.int32)[:, None]
    source = jnp.sum(wanted * jnp.arange(slots, dtype=jnp.int32)[None, :], axis=1)
    return final(recv, source.astype(jnp.int32))


def solution(mesh):
    placed = (
        P(("row", "col"), None, None),
        P(("row", "col"), None),
        P(("row", "col"), None),
        P(("row", "col")),
        P(("row", "col")),
    )
    return jax.shard_map(
        local, mesh=mesh, in_specs=placed, out_specs=P(("row", "col"), None, None), check_vma=False
    )
```

time: 739 us -> 155 us (0.21)
  the two profiles are of different devices: /device:TPU:1 before, /device:TPU:97 now
where the time goes in v1:
time: 155 us; the launch traced here: 154 us
  Pallas kernels  91 us (59%)
  starting transfers between devices  28.4 us (18%)
  waiting for transfers between devices  17.8 us (11%)
  local copies, waits for them, and re-layouts  14.7 us (9%)
  other arithmetic  2.1 us (1%)
    pallas_call x1, Pallas kernels, exchange(): pl.pallas_call(functools.partial(exchange_kernel, slots), out_shape=(jax....  49 us
    ppermute x8, starting transfers between devices, shift(): return lax.ppermute(value, axes, route)  28.4 us
    pallas_call x1, Pallas kernels, coarse_parts(): pl.pallas_call(coarse_kernel, out_shape=jax.ShapeDtypeStruct((3, 6, GW, L...  21.3 us
    ppermute x8, waiting for transfers between devices, shift(): return lax.ppermute(value, axes, route)  17.8 us
    pallas_call x1, Pallas kernels, smooth_rows(): pl.pallas_call(smooth_kernel, out_shape=(jax.ShapeDtypeStruct((R, B, 2 *...  9.23 us
    pallas_call x1, Pallas kernels, assemble(): pl.pallas_call(assemble_kernel, out_shape=jax.ShapeDtypeStruct((slots, 10...  6.65 us
    unnamed x15, local copies, waits for them, and re-layouts  6.43 us
    pallas_call x1, Pallas kernels, final(): pl.pallas_call(final_kernel, out_shape=jax.ShapeDtypeStruct((G, 5 * G, BB...  4.78 us
  transfers between devices with their start and end apart: 8, of which 4 were waited for; matrix products, arithmetic and copies ran while one was open for 4% of the time, Pallas kernels for 0%

profile of v1, /device:TPU:97, one launch (start us, length us, event | category | flops | bytes accessed | tf_op | source)
XLA Modules:
  0.0 154.2 jit_solution(11887998383127846273)
XLA Ops:
  0.0 0.8 fusion.4
  0.8 3.8 %collective-permute-start = (s32[8]{0:T(128)S(1)}, s32[8]{0:T(128)S(1)}, u32[]{:S(2)}, u32[]{:S(2)}) collective-permute-start(s32[8]{0:T(128)S(1)} %get-tuple-element.22), channel_id=1, source_target_pairs={{0,1},{1,2},{2,3},{3,4},{4,5},{5,6},{6,7},{7,8},{8,9},{9,10},{10,1... | collective-permute-start | bytes 104 | tf_op jit(solution)/shard_map/ppermute | solution.py:341
  4.6 1.9 %collective-permute-start.1 = (s32[8]{0:T(128)S(1)}, s32[8]{0:T(128)S(1)}, u32[]{:S(2)}, u32[]{:S(2)}) collective-permute-start(s32[8]{0:T(128)S(1)} %get-tuple-element.23), channel_id=1, source_target_pairs={{1,0},{2,1},{3,2},{4,3},{5,4},{6,5},{7,6},{8,7},{9,8},{10,9},{11,1... | collective-permute-start | bytes 104 | tf_op jit(solution)/shard_map/ppermute | solution.py:341
  6.5 1.0 fusion.3
  7.5 3.6 %collective-permute-start.2 = (f32[8,4096]{1,0:T(8,128)S(1)}, f32[8,4096]{1,0:T(8,128)S(1)}, u32[]{:S(2)}, u32[]{:S(2)}) collective-permute-start(f32[8,4096]{1,0:T(8,128)S(1)} %get-tuple-element.21), channel_id=1, source_target_pairs={{0,1},{1,2},{2,3},{3,4},{4,5},{5,6},{6,7},{7,8},{8,9},{9,10},{10,1... | collective-permute-start | bytes 393224 | tf_op jit(solution)/shard_map/ppermute | solution.py:341
  11.1 2.8 %collective-permute-start.3 = (f32[8,4096]{1,0:T(8,128)S(1)}, f32[8,4096]{1,0:T(8,128)S(1)}, u32[]{:S(2)}, u32[]{:S(2)}) collective-permute-start(f32[8,4096]{1,0:T(8,128)S(1)} %get-tuple-element.20), channel_id=1, source_target_pairs={{1,0},{2,1},{3,2},{4,3},{5,4},{6,5},{7,6},{8,7},{9,8},{10,9},{11,1... | collective-permute-start | bytes 393224 | tf_op jit(solution)/shard_map/ppermute | solution.py:341
  14.0 0.7 subtract_add_fusion
  14.7 0.1 copy.11
  14.8 0.1 reshape.11.cols
  14.9 0.0 copy-start.5
  14.9 0.0 copy-start.2
  14.9 3.8 %copy.12.a_ref = f32[32,6,4096]{2,1,0:T(8,128)S(1)} copy(f32[32,6,4096]{2,0,1:T(8,128)} %param.5) | data formatting | bytes 6291456 | tf_op args[0]
  18.8 0.0 collective-permute-done
  18.8 0.0 collective-permute-done.1
  18.8 0.0 copy-done.5
  18.8 0.1 pad_add_fusion.aggs
  18.9 0.0 collective-permute-done.2.t_low
  18.9 0.0 collective-permute-done.3.t_high
  18.9 0.0 copy-done.2
  18.9 9.2 %smooth.1 = (f32[32,64,512]{2,1,0:T(8,128)S(1)}, bf16[32,6,64,128]{3,2,1,0:T(8,128)(2,1)S(1)}) custom-call(s32[192]{0:T(256)S(1)} %reshape.11.cols, s32[48]{0:T(128)S(1)} %pad_add_fusion.aggs, f32[32,6,4096]{2,1,0:T(8,128)S(1)} %copy.12.a_ref, f32[8,4096]{1,0:T(8,128)S(1)} %collective-permute-done.2.t_low, f32[32,4096]{1,0:T(8,128)S(1)} %copy-done.2, ...), custom_call_target="tpu_custom_call" | custom-call | tf_op jit(solution)/shard_map/smooth/pallas_call | solution.py:98
  28.1 0.0 copy-start.1
  28.1 1.7 %copy-done.1 = bf16[32,6,64,128]{3,2,1,0:T(8,128)(2,1)} copy-done((bf16[32,6,64,128]{3,2,1,0:T(8,128)(2,1)}, bf16[32,6,64,128]{3,2,1,0:T(8,128)(2,1)S(1)}, u32[]{:S(2)}) %copy-start.1) | copy-done | bytes 3145752
  29.8 0.0 copy-start
  29.8 0.2 fusion.2
  30.0 2.7 %collective-permute-start.4 = (f32[8,64,512]{2,1,0:T(8,128)S(1)}, f32[8,64,512]{2,1,0:T(8,128)S(1)}, u32[]{:S(2)}, u32[]{:S(2)}) collective-permute-start(f32[8,64,512]{2,1,0:T(8,128)S(1)} %get-tuple-element.16), channel_id=1, source_target_pairs={{0,1},{1,2},{2,3},{3,4},{4,5},{5,6},{6,7},{7,8},{8,9},{9,10},{10,1... | collective-permute-start | bytes 3145736 | tf_op jit(solution)/shard_map/ppermute | solution.py:341
  32.7 5.0 %collective-permute-start.5 = (f32[8,64,512]{2,1,0:T(8,128)S(1)}, f32[8,64,512]{2,1,0:T(8,128)S(1)}, u32[]{:S(2)}, u32[]{:S(2)}) collective-permute-start(f32[8,64,512]{2,1,0:T(8,128)S(1)} %get-tuple-element.15), channel_id=1, source_target_pairs={{1,0},{2,1},{3,2},{4,3},{5,4},{6,5},{7,6},{8,7},{9,8},{10,9},{11,1... | collective-permute-start | bytes 3145736 | tf_op jit(solution)/shard_map/ppermute | solution.py:341
  37.7 6.8 %collective-permute-done.4.p_low = f32[8,64,512]{2,1,0:T(8,128)S(1)} collective-permute-done((f32[8,64,512]{2,1,0:T(8,128)S(1)}, f32[8,64,512]{2,1,0:T(8,128)S(1)}, u32[]{:S(2)}, u32[]{:S(2)}) %collective-permute-start.4) | collective-permute-done | bytes 1048608 | tf_op jit(solution)/shard_map/ppermute | solution.py:341
  44.5 4.7 %collective-permute-done.5.p_high = f32[8,64,512]{2,1,0:T(8,128)S(1)} collective-permute-done((f32[8,64,512]{2,1,0:T(8,128)S(1)}, f32[8,64,512]{2,1,0:T(8,128)S(1)}, u32[]{:S(2)}, u32[]{:S(2)}) %collective-permute-start.5) | collective-permute-done | bytes 1048608 | tf_op jit(solution)/shard_map/ppermute | solution.py:341
  49.2 0.0 copy-done
  49.2 21.3 %coarse.1 = f32[3,6,256,128]{3,2,1,0:T(8,128)S(1)} custom-call(s32[192]{0:T(256)S(1)} %reshape.11.cols, bf16[32,6,64,128]{3,2,1,0:T(8,128)(2,1)} %copy-done.1, f32[32,64,512]{2,1,0:T(8,128)} %copy-done, f32[8,64,512]{2,1,0:T(8,128)S(1)} %collective-permute-done.4.p_low, f32[8,64,512]{2,1,0:T(8,128)S(1)} %collective-permute-done.5.p_high), custom_call_target="tpu_custom_call" | custom-call | tf_op jit(solution)/shard_map/coarse/pallas_call | solution.py:209
  70.5 0.0 copy-start.6
  70.5 1.1 slice_bitcast_fusion
  71.6 1.9 %collective-permute-start.6 = (f32[6,256,128]{2,1,0:T(8,128)S(1)}, f32[6,256,128]{2,1,0:T(8,128)S(1)}, u32[]{:S(2)}, u32[]{:S(2)}) collective-permute-start(f32[6,256,128]{2,1,0:T(8,128)S(1)} %get-tuple-element.18), channel_id=1, source_target_pairs={{0,1},{1,2},{2,3},{3,4},{4,5},{5,6},{6,7},{7,8},{8,9},{9,10},{10,1... | collective-permute-start | bytes 2359304 | tf_op jit(solution)/shard_map/ppermute | solution.py:341
  73.5 6.6 %collective-permute-start.7 = (f32[6,256,128]{2,1,0:T(8,128)S(1)}, f32[6,256,128]{2,1,0:T(8,128)S(1)}, u32[]{:S(2)}, u32[]{:S(2)}) collective-permute-start(f32[6,256,128]{2,1,0:T(8,128)S(1)} %get-tuple-element.17), channel_id=1, source_target_pairs={{1,0},{2,1},{3,2},{4,3},{5,4},{6,5},{7,6},{8,7},{9,8},{10,9},{11,1... | collective-permute-start | bytes 2359304 | tf_op jit(solution)/shard_map/ppermute | solution.py:341
  80.1 0.0 copy-done.6
  80.2 0.6 select_reduce_fusion.1
  80.8 1.7 %collective-permute-done.6.lower = f32[6,256,128]{2,1,0:T(8,128)S(1)} collective-permute-done((f32[6,256,128]{2,1,0:T(8,128)S(1)}, f32[6,256,128]{2,1,0:T(8,128)S(1)}, u32[]{:S(2)}, u32[]{:S(2)}) %collective-permute-start.6) | collective-permute-done | bytes 786464 | tf_op jit(solution)/shard_map/ppermute | solution.py:341
  82.4 0.0 copy-start.3
  82.4 4.7 %collective-permute-done.7.upper = f32[6,256,128]{2,1,0:T(8,128)S(1)} collective-permute-done((f32[6,256,128]{2,1,0:T(8,128)S(1)}, f32[6,256,128]{2,1,0:T(8,128)S(1)}, u32[]{:S(2)}, u32[]{:S(2)}) %collective-permute-start.7) | collective-permute-done | bytes 786464 | tf_op jit(solution)/shard_map/ppermute | solution.py:341
  87.1 0.0 copy-start.4
  87.1 0.0 copy-done.3
  87.1 0.9 copy-done.4
  88.0 6.7 %assemble.1.send = f32[8,10,64,128]{3,2,1,0:T(8,128)} custom-call(s32[8]{0:T(128)} %get-tuple-element.14.pick, f32[6,256,128]{2,1,0:T(8,128)} %get-tuple-element.19.own, f32[6,256,128]{2,1,0:T(8,128)} %copy-done.3, f32[6,256,128]{2,1,0:T(8,128)} %copy-done.4), custom_call_target="tpu_custom_call" | custom-call | tf_op jit(solution)/shard_map/assemble/pallas_call | solution.py:246
  94.7 0.7 broadcast_in_dim.2.codes
  95.3 49.0 %exchange.1 = (f32[8,10,64,128]{3,2,1,0:T(8,128)}, s32[8,8,128]{2,1,0:T(8,128)}) custom-call(f32[8,10,64,128]{3,2,1,0:T(8,128)} %assemble.1.send, s32[8,8,128]{2,1,0:T(8,128)} %broadcast_in_dim.2.codes), custom_call_target="tpu_custom_call" | custom-call | tf_op jit(solution)/shard_map/exchange/pallas_call | solution.py:297
  144.4 1.0 slice_reduce_fusion
  145.4 0.7 select_reduce_fusion.source
  146.1 4.8 %final.1 = f32[4,20,4096]{2,1,0:T(8,128)} custom-call(s32[4]{0:T(128)} %select_reduce_fusion.source, f32[8,10,64,128]{3,2,1,0:T(8,128)} %get-tuple-element.12.in_ref), custom_call_target="tpu_custom_call" | custom-call | tf_op jit(solution)/shard_map/final/pallas_call | solution.py:323
  150.9 3.3 %copy.13 = f32[4,20,4096]{2,0,1:T(4,128)} copy(f32[4,20,4096]{2,1,0:T(8,128)} %final.1) | data formatting | bytes 2621440 | tf_op jit(solution)/shard_map/final/pallas_call | solution.py:323
  (2 shorter events, 0.0 us)
Async XLA Ops:
  0.8 18.0 %collective-permute-start = (s32[8]{0:T(128)S(1)}, s32[8]{0:T(128)S(1)}, u32[]{:S(2)}, u32[]{:S(2)}) collective-permute-start(s32[8]{0:T(128)S(1)} %get-tuple-element.22), channel_id=1, source_target_pairs={{0,1},{1,2},{2,3},{3,4},{4,5},{5,6},{6,7},{7,8},{8,9},{9,10},{10,1... | collective-permute-start | bytes 104 | tf_op jit(solution)/shard_map/ppermute | solution.py:341
  4.6 14.2 %collective-permute-start.1 = (s32[8]{0:T(128)S(1)}, s32[8]{0:T(128)S(1)}, u32[]{:S(2)}, u32[]{:S(2)}) collective-permute-start(s32[8]{0:T(128)S(1)} %get-tuple-element.23), channel_id=1, source_target_pairs={{1,0},{2,1},{3,2},{4,3},{5,4},{6,5},{7,6},{8,7},{9,8},{10,9},{11,1... | collective-permute-start | bytes 104 | tf_op jit(solution)/shard_map/ppermute | solution.py:341
  7.5 11.4 %collective-permute-start.2 = (f32[8,4096]{1,0:T(8,128)S(1)}, f32[8,4096]{1,0:T(8,128)S(1)}, u32[]{:S(2)}, u32[]{:S(2)}) collective-permute-start(f32[8,4096]{1,0:T(8,128)S(1)} %get-tuple-element.21), channel_id=1, source_target_pairs={{0,1},{1,2},{2,3},{3,4},{4,5},{5,6},{6,7},{7,8},{8,9},{9,10},{10,1... | collective-permute-start | bytes 393224 | tf_op jit(solution)/shard_map/ppermute | solution.py:341
  11.1 7.7 %collective-permute-start.3 = (f32[8,4096]{1,0:T(8,128)S(1)}, f32[8,4096]{1,0:T(8,128)S(1)}, u32[]{:S(2)}, u32[]{:S(2)}) collective-permute-start(f32[8,4096]{1,0:T(8,128)S(1)} %get-tuple-element.20), channel_id=1, source_target_pairs={{1,0},{2,1},{3,2},{4,3},{5,4},{6,5},{7,6},{8,7},{9,8},{10,9},{11,1... | collective-permute-start | bytes 393224 | tf_op jit(solution)/shard_map/ppermute | solution.py:341
  14.9 3.9 %copy-start.5 = (s32[32]{0:T(128)S(1)}, s32[32]{0:T(128)}, u32[]{:S(2)}) copy-start(s32[32]{0:T(128)} %param.8) | copy-start | bytes 388
  14.9 4.0 %copy-start.2 = (f32[32,4096]{1,0:T(8,128)S(1)}, f32[32,4096]{1,0:T(8,128)}, u32[]{:S(2)}) copy-start(f32[32,4096]{1,0:T(8,128)} %t_own.1) | copy-start | bytes 1572868
  28.1 1.7 %copy-start.1 = (bf16[32,6,64,128]{3,2,1,0:T(8,128)(2,1)}, bf16[32,6,64,128]{3,2,1,0:T(8,128)(2,1)S(1)}, u32[]{:S(2)}) copy-start(bf16[32,6,64,128]{3,2,1,0:T(8,128)(2,1)S(1)} %get-tuple-element.9.aa_ref) | copy-start | bytes 9437188
  29.8 19.4 %copy-start = (f32[32,64,512]{2,1,0:T(8,128)}, f32[32,64,512]{2,1,0:T(8,128)S(1)}, u32[]{:S(2)}) copy-start(f32[32,64,512]{2,1,0:T(8,128)S(1)} %get-tuple-element.10.p_own) | copy-start | bytes 12582916
  30.0 14.5 %collective-permute-start.4 = (f32[8,64,512]{2,1,0:T(8,128)S(1)}, f32[8,64,512]{2,1,0:T(8,128)S(1)}, u32[]{:S(2)}, u32[]{:S(2)}) collective-permute-start(f32[8,64,512]{2,1,0:T(8,128)S(1)} %get-tuple-element.16), channel_id=1, source_target_pairs={{0,1},{1,2},{2,3},{3,4},{4,5},{5,6},{6,7},{7,8},{8,9},{9,10},{10,1... | collective-permute-start | bytes 3145736 | tf_op jit(solution)/shard_map/ppermute | solution.py:341
  32.7 16.4 %collective-permute-start.5 = (f32[8,64,512]{2,1,0:T(8,128)S(1)}, f32[8,64,512]{2,1,0:T(8,128)S(1)}, u32[]{:S(2)}, u32[]{:S(2)}) collective-permute-start(f32[8,64,512]{2,1,0:T(8,128)S(1)} %get-tuple-element.15), channel_id=1, source_target_pairs={{1,0},{2,1},{3,2},{4,3},{5,4},{6,5},{7,6},{8,7},{9,8},{10,9},{11,1... | collective-permute-start | bytes 3145736 | tf_op jit(solution)/shard_map/ppermute | solution.py:341
  70.5 9.6 %copy-start.6 = (s32[4]{0:T(128)S(1)}, s32[4]{0:T(128)}, u32[]{:S(2)}) copy-start(s32[4]{0:T(128)} %param.9) | copy-start | bytes 52
  71.6 10.8 %collective-permute-start.6 = (f32[6,256,128]{2,1,0:T(8,128)S(1)}, f32[6,256,128]{2,1,0:T(8,128)S(1)}, u32[]{:S(2)}, u32[]{:S(2)}) collective-permute-start(f32[6,256,128]{2,1,0:T(8,128)S(1)} %get-tuple-element.18), channel_id=1, source_target_pairs={{0,1},{1,2},{2,3},{3,4},{4,5},{5,6},{6,7},{7,8},{8,9},{9,10},{10,1... | collective-permute-start | bytes 2359304 | tf_op jit(solution)/shard_map/ppermute | solution.py:341
  73.5 13.6 %collective-permute-start.7 = (f32[6,256,128]{2,1,0:T(8,128)S(1)}, f32[6,256,128]{2,1,0:T(8,128)S(1)}, u32[]{:S(2)}, u32[]{:S(2)}) collective-permute-start(f32[6,256,128]{2,1,0:T(8,128)S(1)} %get-tuple-element.17), channel_id=1, source_target_pairs={{1,0},{2,1},{3,2},{4,3},{5,4},{6,5},{7,6},{8,7},{9,8},{10,9},{11,1... | collective-permute-start | bytes 2359304 | tf_op jit(solution)/shard_map/ppermute | solution.py:341
  82.4 4.7 %copy-start.3 = (f32[6,256,128]{2,1,0:T(8,128)}, f32[6,256,128]{2,1,0:T(8,128)S(1)}, u32[]{:S(2)}) copy-start(f32[6,256,128]{2,1,0:T(8,128)S(1)} %collective-permute-done.6.lower) | copy-start | bytes 2359300
  87.1 0.9 copy-start.4

commit v2 on v1

--- a/solution.py
+++ b/solution.py
@@ -33,7 +33,7 @@
 
 def smooth_kernel(cols, aggs, a_ref, t_low, t_own, t_high, p_ref, aa_ref, flat, nat, t_nat, t_split):
     step = pl.program_id(0)
-    rows = a_ref.shape[0]
+    rows = 8
     low = lane_low(B)
 
     @pl.when(step == 0)
@@ -61,15 +61,15 @@
 
     for r in range(rows):
         n = step * rows + r
-        for c in range(B // 2):
-            flat[pl.ds(c * 8, K), :] = a_ref[r, :, c * LANES : (c + 1) * LANES]
         for part in range(4):
             p_ref[r, :, part * LANES : (part + 1) * LANES] = jnp.zeros((B, LANES), f32)
         scale = None
         for k in range(K):
             ci = cols[n * K + k]
-            natural_dup(flat[pl.ds(k, B // 2, stride=8), :], nat.at[k % 2])
-            value = nat[k % 2]
+            tiles = a_ref.at[k, 0].reshape(B // 2 * 8, LANES)
+            slot = (r % 2) * K + k
+            natural_dup(tiles[pl.ds(r, B // 2, stride=8), :], nat.at[slot])
+            value = nat[slot]
             if k == 0:
                 diagonal = jnp.sum(jnp.where(on_diagonal, value, 0.0), axis=1, keepdims=True)
                 scale = relaxation / diagonal
@@ -93,7 +93,8 @@
 
 
 def smooth_rows(a_blocks, t_low, t_own, t_high, cols, aggs):
-    rows = 4
+    rows = 8
+    tiled = a_blocks.reshape(R // rows, rows, K, B // 2, LANES).transpose(2, 0, 3, 1, 4)
     whole = lambda shape: pl.BlockSpec(shape, lambda i, *_: (0,) * len(shape))
     return pl.pallas_call(
         smooth_kernel,
@@ -105,7 +106,7 @@
             num_scalar_prefetch=2,
             grid=(R // rows,),
             in_specs=[
-                pl.BlockSpec((rows, K, BB), lambda i, *_: (i, 0, 0)),
+                pl.BlockSpec((K, 1, B // 2, rows, LANES), lambda i, *_: (0, i, 0, 0, 0)),
                 whole((H, BB)),
                 whole((R, BB)),
                 whole((H, BB)),
@@ -116,14 +117,14 @@
             ),
             scratch_shapes=[
                 pltpu.VMEM((B // 2 * 8, LANES), f32),
-                pltpu.VMEM((2, B, LANES), f32),
+                pltpu.VMEM((2 * K, B, LANES), f32),
                 pltpu.VMEM((R + 2 * H, B, LANES), f32),
                 pltpu.VMEM((R + 2 * H, 2 * B, LANES), bf16),
             ],
         ),
         compiler_params=pltpu.CompilerParams(vmem_limit_bytes=40 << 20),
         name="smooth",
-    )(cols, aggs, a_blocks, t_low, t_own, t_high)
+    )(cols, aggs, tiled, t_low, t_own, t_high)
 
 
 def coarse_kernel(cols, aa_ref, p_own, p_low, p_high, out_ref, p_split, ap):
@@ -190,7 +191,8 @@
             value = value + product(p_low_part[:, lanes], high)
             value = value + product(p_high_part[:, lanes], low)
             for half in range(2):
-                out_ref[target, 2 * g + half] += value[:, half * LANES : (half + 1) * LANES]
+                tile = value[:, half * LANES : (half + 1) * LANES]
+                out_ref[target, :, 2 * g + half] += tile.reshape(G, B, LANES)
 
     add(1, slice(0, GW))
 
@@ -208,7 +210,7 @@
     whole = lambda shape: pl.BlockSpec(shape, lambda i, *_: (0,) * len(shape))
     return pl.pallas_call(
         coarse_kernel,
-        out_shape=jax.ShapeDtypeStruct((3, 6, GW, LANES), f32),
+        out_shape=jax.ShapeDtypeStruct((3, G, 6, B, LANES), f32),
         grid_spec=pltpu.PrefetchScalarGridSpec(
             num_scalar_prefetch=1,
             grid=(R // rows,),
@@ -218,7 +220,7 @@
                 whole((H, B, 2 * GW)),
                 whole((H, B, 2 * GW)),
             ],
-            out_specs=whole((3, 6, GW, LANES)),
+            out_specs=whole((3, G, 6, B, LANES)),
             scratch_shapes=[
                 pltpu.VMEM((R + 2 * H, 2 * B, 2 * GW), bf16),
                 pltpu.VMEM((3, rows * B, GW), f32),
@@ -229,109 +231,155 @@
     )(cols, pieces, p_own, p_low, p_high)
 
 
-def assemble_kernel(pick, own, lower, upper, out_ref):
-    for j in range(10):
-        terms = []
-        if j < 6:
-            terms.append(lower[j])
-        if 2 <= j < 8:
-            terms.append(own[j - 2])
-        if j >= 4:
-            terms.append(upper[j - 4])
-        out_ref[0, j] = functools.reduce(jnp.add, terms)
-
-
-def assemble(own, lower, upper, pick, slots):
-    spec = pl.BlockSpec((6, B, LANES), lambda j, pick: (0, pick[j], 0))
-    return pl.pallas_call(
-        assemble_kernel,
-        out_shape=jax.ShapeDtypeStruct((slots, 10, B, LANES), f32),
-        grid_spec=pltpu.PrefetchScalarGridSpec(
-            num_scalar_prefetch=1,
-            grid=(slots,),
-            in_specs=[spec, spec, spec],
-            out_specs=pl.BlockSpec((1, 10, B, LANES), lambda j, pick: (j, 0, 0, 0)),
-        ),
-        name="assemble",
-    )(pick, own, lower, upper)
-
-
-def exchange_kernel(slots, send, codes, recv, got, send_sem, recv_sem, code_send, code_recv, own_sem):
-    me = lax.axis_index("col")
-    row = lax.axis_index("row")
+MESH = pl.DeviceIdType.MESH
+CHUNKS = 5
+
+
+def finish_kernel(
+    slots, pick, codes, parts, recv, got, lower, upper, send, relay,
+    near_send, near_recv, code_send, code_recv, send_sem, recv_sem, hop_send, hop_recv, own_sem,
+):
+    me, row = lax.axis_index("col"), lax.axis_index("row")
+    rows = lax.axis_size("row")
+    device, count = row * slots + me, rows * slots
+
+    def place(index):
+        return (index // slots, lax.rem(index, slots))
+
+    behind = place(lax.rem(device + count - 1, count))
+    ahead = place(lax.rem(device + 1, count))
+    peers = [lax.rem(me + s, slots) for s in range(1, slots)]
     barrier = pltpu.get_barrier_semaphore()
-    for s in range(1, slots):
-        peer = lax.rem(me + s, slots)
-        pl.semaphore_signal(
-            barrier, inc=1, device_id=(row, peer), device_id_type=pl.DeviceIdType.MESH
+    targets = [(row, peer) for peer in peers] + [behind, ahead]
+    for target in targets:
+        pl.semaphore_signal(barrier, inc=1, device_id=target, device_id_type=MESH)
+    pl.semaphore_wait(barrier, len(targets))
+
+    def remote(source, target, here, there, where):
+        copy = pltpu.make_async_remote_copy(
+            src_ref=source, dst_ref=target, send_sem=here, recv_sem=there,
+            device_id=where, device_id_type=MESH,
         )
-    pl.semaphore_wait(barrier, slots - 1)
+        copy.start()
+        return copy
+
+    near = [
+        remote(parts.at[2], lower, near_send.at[0], near_recv.at[0], ahead),
+        remote(parts.at[0], upper, near_send.at[1], near_recv.at[1], behind),
+    ]
     copies = []
-    for s in range(1, slots):
-        peer = lax.rem(me + s, slots)
-        for source, target, here, there in (
-            (codes, got, code_send, code_recv),
-            (send, recv, send_sem, recv_sem),
-        ):
-            copy = pltpu.make_async_remote_copy(
-                src_ref=source.at[peer],
-                dst_ref=target.at[me],
-                send_sem=here.at[s],
-                recv_sem=there.at[s],
-                device_id=(row, peer),
-                device_id_type=pl.DeviceIdType.MESH,
-            )
-            copy.start()
-            copies.append(copy)
+    for s, peer in enumerate(peers):
+        copies.append(
+            remote(codes.at[peer], got.at[me], code_send.at[s], code_recv.at[s], (row, peer))
+        )
+    for copy in near:
+        copy.wait_recv()
+
+    has_low = (device > 0).astype(f32)
+    has_high = (device < count - 1).astype(f32)
+
+    def build(target):
+        a = pick[target]
+        for j in range(10):
+            terms = []
+            if j < 6:
+                terms.append(lower[a, j] * has_low)
+            if 2 <= j < 8:
+                terms.append(parts[1, a, j - 2])
+            if j >= 4:
+                terms.append(upper[a, j - 4] * has_high)
+            send[target, j] = functools.reduce(jnp.add, terms)
+
+    core = lax.rem(me, 2)
+    chip = me - core
+    far = lax.rem(chip + 4, slots)
+    before = lax.rem(chip + 6, slots)
+    after = lax.rem(chip + 2, slots)
+    step = 10 // CHUNKS
+    order = [far + core, far + 1 - core, after + core, before + core, after + 1 - core, before + 1 - core, chip + 1 - core]
+    for s, peer in enumerate(order):
+        build(peer)
+        copies.append(
+            remote(send.at[peer], recv.at[me], send_sem.at[s], recv_sem.at[s], (row, peer))
+        )
+    build(me)
     for index, (source, target) in enumerate(((codes, got), (send, recv))):
         copy = pltpu.make_async_copy(source.at[me], target.at[me], own_sem.at[index])
         copy.start()
         copies.append(copy)
-    for copy in copies:
+    hops, last = [], []
+    for copy in near + hops:
+        copy.wait_send()
+    for copy in copies + last:
         copy.wait()
 
 
-def exchange(send, codes, slots):
+def finish(parts, pick, codes, slots):
     anywhere = pl.BlockSpec(memory_space=pl.ANY)
+    vmem = pl.BlockSpec(memory_space=pltpu.VMEM)
     dma = pltpu.SemaphoreType.DMA
     return pl.pallas_call(
-        functools.partial(exchange_kernel, slots),
+        functools.partial(finish_kernel, slots),
         out_shape=(
-            jax.ShapeDtypeStruct(send.shape, send.dtype),
+            jax.ShapeDtypeStruct((slots, 10, B, LANES), f32),
             jax.ShapeDtypeStruct(codes.shape, codes.dtype),
         ),
-        in_specs=[anywhere, anywhere],
-        out_specs=(anywhere, anywhere),
-        scratch_shapes=[dma((slots,)), dma((slots,)), dma((slots,)), dma((slots,)), dma((2,))],
-        compiler_params=pltpu.CompilerParams(collective_id=0, has_side_effects=True),
-        name="exchange",
-    )(send, codes)
-
-
-def final_kernel(source, in_ref, out_ref, pairs):
+        in_specs=[pl.BlockSpec(memory_space=pltpu.SMEM), vmem, vmem],
+        out_specs=(anywhere, vmem),
+        scratch_shapes=[
+            pltpu.VMEM((G, 6, B, LANES), f32),
+            pltpu.VMEM((G, 6, B, LANES), f32),
+            pltpu.VMEM((slots, 10, B, LANES), f32),
+            pltpu.VMEM((10, B, LANES), f32),
+            dma((2,)), dma((2,)),
+            dma((slots,)), dma((slots,)),
+            dma((slots,)), dma((slots,)),
+            dma((2 * CHUNKS,)), dma((2 * CHUNKS,)),
+            dma((2,)),
+        ],
+        compiler_params=pltpu.CompilerParams(
+            collective_id=0, has_side_effects=True, vmem_limit_bytes=32 << 20
+        ),
+        name="finish",
+    )(pick, codes, parts)
+
+
+def final_kernel(source, *refs):
+    blocks, out_ref, pairs = refs[:G], refs[G], refs[G + 1]
     low = lane_low(B // 2)
-    for j in range(5 * G // 2):
-        even = in_ref[0, j, pl.ds(0, B // 2, stride=2), :]
-        odd = in_ref[0, j, pl.ds(1, B // 2, stride=2), :]
-        pairs[pl.ds(2 * j * (B // 2), B // 2), :] = jnp.where(low, even, pltpu.roll(odd, B, 1))
-        pairs[pl.ds((2 * j + 1) * (B // 2), B // 2), :] = jnp.where(low, pltpu.roll(even, B, 1), odd)
-    for c in range(B // 2):
-        out_ref[0, :, c * LANES : (c + 1) * LANES] = pairs[pl.ds(c, 5 * G, stride=B // 2), :]
+    tiles = blocks[0].shape[1]
+    for g in range(G):
+        for j in range(tiles):
+            even = blocks[g][0, j, pl.ds(0, B // 2, stride=2), :]
+            odd = blocks[g][0, j, pl.ds(1, B // 2, stride=2), :]
+            base = (g * tiles + j) * B
+            pairs[pl.ds(base, B // 2), :] = jnp.where(low, even, pltpu.roll(odd, B, 1))
+            pairs[pl.ds(base + B // 2, B // 2), :] = jnp.where(low, pltpu.roll(even, B, 1), odd)
+    for col in range(2 * tiles):
+        for c in range(B // 2):
+            rows = pl.ds(col * (B // 2) + c, G, stride=tiles * B)
+            out_ref[col, :, c * LANES : (c + 1) * LANES] = pairs[rows, :]
 
 
 def final(recv, source):
-    return pl.pallas_call(
+    tiles = 2
+    specs = [
+        pl.BlockSpec((1, tiles, B, LANES), lambda j, source, g=g: (source[g], j, 0, 0))
+        for g in range(G)
+    ]
+    result = pl.pallas_call(
         final_kernel,
-        out_shape=jax.ShapeDtypeStruct((G, 5 * G, BB), f32),
+        out_shape=jax.ShapeDtypeStruct((5 * G, G, BB), f32),
         grid_spec=pltpu.PrefetchScalarGridSpec(
             num_scalar_prefetch=1,
-            grid=(G,),
-            in_specs=[pl.BlockSpec((1, 10, B, LANES), lambda g, source: (source[g], 0, 0, 0))],
-            out_specs=pl.BlockSpec((1, 5 * G, BB), lambda g, source: (g, 0, 0)),
-            scratch_shapes=[pltpu.VMEM((5 * G * B // 2, LANES), f32)],
+            grid=(10 // tiles,),
+            in_specs=specs,
+            out_specs=pl.BlockSpec((2 * tiles, G, BB), lambda j, source: (j, 0, 0)),
+            scratch_shapes=[pltpu.VMEM((G * tiles * B, LANES), f32)],
         ),
         name="final",
-    )(source, recv)
+    )(source, recv, recv, recv, recv)
+    return result.transpose(1, 0, 2)
 
 
 def shift(value, distance):
@@ -351,15 +399,12 @@
     p_own, pieces = smooth_rows(a_blocks, t_low, tentative, t_high, cols, aggs)
     p_low, p_high = shift(p_own[R - H :], 1), shift(p_own[:H], -1)
     parts = coarse_parts(pieces, p_own, p_low, p_high, cols)
-    from_lower, from_upper = shift(parts[2], 1), shift(parts[0], -1)
-
     target = (owner // G) % slots
     hits = target[None, :] == jnp.arange(slots, dtype=jnp.int32)[:, None]
     pick = jnp.sum(hits * jnp.arange(G, dtype=jnp.int32)[None, :], axis=1).astype(jnp.int32)
     place = jnp.sum(hits * (owner % G + 1)[None, :], axis=1).astype(jnp.int32)
     codes = jnp.broadcast_to(place[:, None, None], (slots, 8, LANES))
-    send = assemble(parts[1], from_lower, from_upper, pick, slots)
-    recv, got = exchange(send, codes, slots)
+    recv, got = finish(parts, pick, codes, slots)
     places = got[:, 0, 0]
     wanted = places[None, :] == jnp.arange(1, G + 1, dtype=jnp.int32)[:, None]
     source = jnp.sum(wanted * jnp.arange(slots, dtype=jnp.int32)[None, :], axis=1)

time: 155 us -> 138 us (0.89)
  the two profiles are of different devices: /device:TPU:97 before, /device:TPU:1 now
where the time goes in v2:
time: 138 us; the launch traced here: 137 us
  Pallas kernels  93.6 us (68%)
  starting transfers between devices  16.5 us (12%)
  waiting for transfers between devices  16.2 us (12%)
  local copies, waits for them, and re-layouts  8.63 us (6%)
  other arithmetic  2.31 us (2%)
    pallas_call x1, Pallas kernels, finish(): pl.pallas_call(functools.partial(finish_kernel, slots), out_shape=(jax.Sh...  57.5 us
    pallas_call x1, Pallas kernels, coarse_parts(): pl.pallas_call(coarse_kernel, out_shape=jax.ShapeDtypeStruct((3, G, 6, B,...  21.3 us
    ppermute x6, starting transfers between devices, shift(): return lax.ppermute(value, axes, route)  16.5 us
    ppermute x6, waiting for transfers between devices, shift(): return lax.ppermute(value, axes, route)  16.2 us
    pallas_call x1, Pallas kernels, smooth_rows(): pl.pallas_call(smooth_kernel, out_shape=(jax.ShapeDtypeStruct((R, B, 2 *...  9.34 us
    unnamed x12, local copies, waits for them, and re-layouts  6.12 us
    pallas_call x1, Pallas kernels, final(): pl.pallas_call(final_kernel, out_shape=jax.ShapeDtypeStruct((5 * G, G, BB...  5.34 us
  transfers between devices with their start and end apart: 6, of which 3 were waited for; matrix products, arithmetic and copies ran while one was open for 2% of the time, Pallas kernels for 0%

profile of v2, /device:TPU:1, one launch (start us, length us, event | category | flops | bytes accessed | tf_op | source)
XLA Modules:
  0.0 137.3 jit_solution(11554873872507208261)
XLA Ops:
  0.0 0.8 fusion.4
  0.8 4.6 %collective-permute-start = (s32[8]{0:T(128)S(1)}, s32[8]{0:T(128)S(1)}, u32[]{:S(2)}, u32[]{:S(2)}) collective-permute-start(s32[8]{0:T(128)S(1)} %get-tuple-element.19), channel_id=1, source_target_pairs={{0,1},{1,2},{2,3},{3,4},{4,5},{5,6},{6,7},{7,8},{8,9},{9,10},{10,1... | collective-permute-start | bytes 104 | tf_op jit(solution)/shard_map/ppermute | solution.py:389
  5.4 1.9 %collective-permute-start.1 = (s32[8]{0:T(128)S(1)}, s32[8]{0:T(128)S(1)}, u32[]{:S(2)}, u32[]{:S(2)}) collective-permute-start(s32[8]{0:T(128)S(1)} %get-tuple-element.20), channel_id=1, source_target_pairs={{1,0},{2,1},{3,2},{4,3},{5,4},{6,5},{7,6},{8,7},{9,8},{10,9},{11,1... | collective-permute-start | bytes 104 | tf_op jit(solution)/shard_map/ppermute | solution.py:389
  7.3 1.0 fusion.3
  8.3 3.6 %collective-permute-start.2 = (f32[8,4096]{1,0:T(8,128)S(1)}, f32[8,4096]{1,0:T(8,128)S(1)}, u32[]{:S(2)}, u32[]{:S(2)}) collective-permute-start(f32[8,4096]{1,0:T(8,128)S(1)} %get-tuple-element.18), channel_id=1, source_target_pairs={{0,1},{1,2},{2,3},{3,4},{4,5},{5,6},{6,7},{7,8},{8,9},{9,10},{10,1... | collective-permute-start | bytes 393224 | tf_op jit(solution)/shard_map/ppermute | solution.py:389
  12.0 1.9 %collective-permute-start.3 = (f32[8,4096]{1,0:T(8,128)S(1)}, f32[8,4096]{1,0:T(8,128)S(1)}, u32[]{:S(2)}, u32[]{:S(2)}) collective-permute-start(f32[8,4096]{1,0:T(8,128)S(1)} %get-tuple-element.17), channel_id=1, source_target_pairs={{1,0},{2,1},{3,2},{4,3},{5,4},{6,5},{7,6},{8,7},{9,8},{10,9},{11,1... | collective-permute-start | bytes 393224 | tf_op jit(solution)/shard_map/ppermute | solution.py:389
  13.9 0.7 subtract_add_fusion
  14.6 0.1 copy.7
  14.7 0.1 reshape.14.cols
  14.8 0.0 collective-permute-done
  14.8 0.0 collective-permute-done.1
  14.8 0.7 pad_add_fusion.aggs
  15.5 0.0 collective-permute-done.2.t_low
  15.5 2.7 %collective-permute-done.3.t_high = f32[8,4096]{1,0:T(8,128)S(1)} collective-permute-done((f32[8,4096]{1,0:T(8,128)S(1)}, f32[8,4096]{1,0:T(8,128)S(1)}, u32[]{:S(2)}, u32[]{:S(2)}) %collective-permute-start.3) | collective-permute-done | bytes 131104 | tf_op jit(solution)/shard_map/ppermute | solution.py:389
  18.3 0.0 copy-start.2
  18.3 1.9 %copy-done.2 = f32[32,6,4096]{2,0,1:T(8,128)S(1)} copy-done((f32[32,6,4096]{2,0,1:T(8,128)S(1)}, f32[32,6,4096]{2,0,1:T(8,128)}, u32[]{:S(2)}) %copy-start.2) | copy-done | bytes 3145752
  20.1 0.0 copy-start.4
  20.1 1.0 copy-done.4
  21.2 0.0 copy-start.5
  21.2 9.3 %smooth.1 = (f32[32,64,512]{2,1,0:T(8,128)S(1)}, bf16[32,6,64,128]{3,2,1,0:T(8,128)(2,1)S(1)}) custom-call(s32[192]{0:T(256)S(1)} %reshape.14.cols, s32[48]{0:T(128)S(1)} %pad_add_fusion.aggs, f32[6,4,32,8,128]{4,3,2,1,0:T(8,128)S(1)} %bitcast.4, f32[8,4096]{1,0:T(8,128)S(1)} %collective-permute-done.2.t_low, f32[32,4096]{1,0:T(8,128)S(1)} %copy-done.4, ...), custom_call_target="tpu_custom_call" | custom-call | tf_op jit(solution)/shard_map/smooth/pallas_call | solution.py:99
  30.5 0.0 copy-start.3
  30.5 1.7 %copy-done.3 = bf16[32,6,64,128]{3,2,1,0:T(8,128)(2,1)} copy-done((bf16[32,6,64,128]{3,2,1,0:T(8,128)(2,1)}, bf16[32,6,64,128]{3,2,1,0:T(8,128)(2,1)S(1)}, u32[]{:S(2)}) %copy-start.3) | copy-done | bytes 3145752
  32.2 0.0 copy-start.1
  32.2 0.2 fusion.2
  32.4 1.9 %collective-permute-start.4 = (f32[8,64,512]{2,1,0:T(8,128)S(1)}, f32[8,64,512]{2,1,0:T(8,128)S(1)}, u32[]{:S(2)}, u32[]{:S(2)}) collective-permute-start(f32[8,64,512]{2,1,0:T(8,128)S(1)} %get-tuple-element.16), channel_id=1, source_target_pairs={{0,1},{1,2},{2,3},{3,4},{4,5},{5,6},{6,7},{7,8},{8,9},{9,10},{10,1... | collective-permute-start | bytes 3145736 | tf_op jit(solution)/shard_map/ppermute | solution.py:389
  34.4 2.5 %collective-permute-start.5 = (f32[8,64,512]{2,1,0:T(8,128)S(1)}, f32[8,64,512]{2,1,0:T(8,128)S(1)}, u32[]{:S(2)}, u32[]{:S(2)}) collective-permute-start(f32[8,64,512]{2,1,0:T(8,128)S(1)} %get-tuple-element.15), channel_id=1, source_target_pairs={{1,0},{2,1},{3,2},{4,3},{5,4},{6,5},{7,6},{8,7},{9,8},{10,9},{11,1... | collective-permute-start | bytes 3145736 | tf_op jit(solution)/shard_map/ppermute | solution.py:389
  36.9 0.0 copy-done.5
  36.9 0.1 select_reduce_fusion.1
  37.0 9.1 %collective-permute-done.4.p_low = f32[8,64,512]{2,1,0:T(8,128)S(1)} collective-permute-done((f32[8,64,512]{2,1,0:T(8,128)S(1)}, f32[8,64,512]{2,1,0:T(8,128)S(1)}, u32[]{:S(2)}, u32[]{:S(2)}) %collective-permute-start.4) | collective-permute-done | bytes 1048608 | tf_op jit(solution)/shard_map/ppermute | solution.py:389
  46.1 4.4 %collective-permute-done.5.p_high = f32[8,64,512]{2,1,0:T(8,128)S(1)} collective-permute-done((f32[8,64,512]{2,1,0:T(8,128)S(1)}, f32[8,64,512]{2,1,0:T(8,128)S(1)}, u32[]{:S(2)}, u32[]{:S(2)}) %collective-permute-start.5) | collective-permute-done | bytes 1048608 | tf_op jit(solution)/shard_map/ppermute | solution.py:389
  50.5 0.0 copy-done.1
  50.5 21.3 %coarse.1.parts = f32[3,4,6,64,128]{4,3,2,1,0:T(8,128)S(1)} custom-call(s32[192]{0:T(256)S(1)} %reshape.14.cols, bf16[32,6,64,128]{3,2,1,0:T(8,128)(2,1)} %copy-done.3, f32[32,64,512]{2,1,0:T(8,128)} %copy-done.1, f32[8,64,512]{2,1,0:T(8,128)S(1)} %collective-permute-done.4.p_low, f32[8,64,512]{2,1,0:T(8,128)S(1)} %collective-permute-done.5.p_high), custom_call_target="tpu_custom_call" | custom-call | tf_op jit(solution)/shard_map/coarse/pallas_call | solution.py:211
  71.8 0.1 broadcast_in_dim.2.codes
  71.9 57.5 %finish.1 = (f32[8,10,64,128]{3,2,1,0:T(8,128)S(1)}, s32[8,8,128]{2,1,0:T(8,128)S(1)}) custom-call(s32[8]{0:T(128)S(1)} %get-tuple-element.14.pick, s32[8,8,128]{2,1,0:T(8,128)S(1)} %broadcast_in_dim.2.codes, f32[3,4,6,64,128]{4,3,2,1,0:T(8,128)S(1)} %coarse.1.parts), custom_call_target="tpu_custom_call" | custom-call | tf_op jit(solution)/shard_map/finish/pallas_call | solution.py:321
  129.5 0.0 copy-start
  129.5 1.5 %copy-done = f32[8,10,64,128]{3,2,1,0:T(8,128)} copy-done((f32[8,10,64,128]{3,2,1,0:T(8,128)}, f32[8,10,64,128]{3,2,1,0:T(8,128)S(1)}, u32[]{:S(2)}) %copy-start) | copy-done | bytes 2621464
  131.0 0.2 slice_reduce_fusion
  131.2 0.8 select_reduce_fusion.source
  132.0 5.3 %final.1 = f32[20,4,4096]{2,1,0:T(4,128)} custom-call(s32[4]{0:T(128)} %select_reduce_fusion.source, f32[8,10,64,128]{3,2,1,0:T(8,128)} %copy-done, f32[8,10,64,128]{3,2,1,0:T(8,128)} %copy-done, f32[8,10,64,128]{3,2,1,0:T(8,128)} %copy-done, f32[8,10,64,128]{3,2,1,0:T(8,128)} %copy-done), custom_call_target="tpu_custom_call" | custom-call | tf_op jit(solution)/shard_map/final/pallas_call | solution.py:370
  (2 shorter events, 0.0 us)
Async XLA Ops:
  0.8 14.0 %collective-permute-start = (s32[8]{0:T(128)S(1)}, s32[8]{0:T(128)S(1)}, u32[]{:S(2)}, u32[]{:S(2)}) collective-permute-start(s32[8]{0:T(128)S(1)} %get-tuple-element.19), channel_id=1, source_target_pairs={{0,1},{1,2},{2,3},{3,4},{4,5},{5,6},{6,7},{7,8},{8,9},{9,10},{10,1... | collective-permute-start | bytes 104 | tf_op jit(solution)/shard_map/ppermute | solution.py:389
  5.4 9.4 %collective-permute-start.1 = (s32[8]{0:T(128)S(1)}, s32[8]{0:T(128)S(1)}, u32[]{:S(2)}, u32[]{:S(2)}) collective-permute-start(s32[8]{0:T(128)S(1)} %get-tuple-element.20), channel_id=1, source_target_pairs={{1,0},{2,1},{3,2},{4,3},{5,4},{6,5},{7,6},{8,7},{9,8},{10,9},{11,1... | collective-permute-start | bytes 104 | tf_op jit(solution)/shard_map/ppermute | solution.py:389
  8.3 7.2 %collective-permute-start.2 = (f32[8,4096]{1,0:T(8,128)S(1)}, f32[8,4096]{1,0:T(8,128)S(1)}, u32[]{:S(2)}, u32[]{:S(2)}) collective-permute-start(f32[8,4096]{1,0:T(8,128)S(1)} %get-tuple-element.18), channel_id=1, source_target_pairs={{0,1},{1,2},{2,3},{3,4},{4,5},{5,6},{6,7},{7,8},{8,9},{9,10},{10,1... | collective-permute-start | bytes 393224 | tf_op jit(solution)/shard_map/ppermute | solution.py:389
  12.0 6.3 %collective-permute-start.3 = (f32[8,4096]{1,0:T(8,128)S(1)}, f32[8,4096]{1,0:T(8,128)S(1)}, u32[]{:S(2)}, u32[]{:S(2)}) collective-permute-start(f32[8,4096]{1,0:T(8,128)S(1)} %get-tuple-element.17), channel_id=1, source_target_pairs={{1,0},{2,1},{3,2},{4,3},{5,4},{6,5},{7,6},{8,7},{9,8},{10,9},{11,1... | collective-permute-start | bytes 393224 | tf_op jit(solution)/shard_map/ppermute | solution.py:389
  18.3 1.9 %copy-start.2 = (f32[32,6,4096]{2,0,1:T(8,128)S(1)}, f32[32,6,4096]{2,0,1:T(8,128)}, u32[]{:S(2)}) copy-start(f32[32,6,4096]{2,0,1:T(8,128)} %param.5) | copy-start | bytes 9437188
  20.1 1.0 copy-start.4
  21.2 15.7 %copy-start.5 = (s32[4]{0:T(128)S(1)}, s32[4]{0:T(128)}, u32[]{:S(2)}) copy-start(s32[4]{0:T(128)} %param.9) | copy-start | bytes 52
  30.5 1.7 %copy-start.3 = (bf16[32,6,64,128]{3,2,1,0:T(8,128)(2,1)}, bf16[32,6,64,128]{3,2,1,0:T(8,128)(2,1)S(1)}, u32[]{:S(2)}) copy-start(bf16[32,6,64,128]{3,2,1,0:T(8,128)(2,1)S(1)} %get-tuple-element.9.aa_ref) | copy-start | bytes 9437188
  32.2 18.3 %copy-start.1 = (f32[32,64,512]{2,1,0:T(8,128)}, f32[32,64,512]{2,1,0:T(8,128)S(1)}, u32[]{:S(2)}) copy-start(f32[32,64,512]{2,1,0:T(8,128)S(1)} %get-tuple-element.10.p_own) | copy-start | bytes 12582916
  32.4 13.7 %collective-permute-start.4 = (f32[8,64,512]{2,1,0:T(8,128)S(1)}, f32[8,64,512]{2,1,0:T(8,128)S(1)}, u32[]{:S(2)}, u32[]{:S(2)}) collective-permute-start(f32[8,64,512]{2,1,0:T(8,128)S(1)} %get-tuple-element.16), channel_id=1, source_target_pairs={{0,1},{1,2},{2,3},{3,4},{4,5},{5,6},{6,7},{7,8},{8,9},{9,10},{10,1... | collective-permute-start | bytes 3145736 | tf_op jit(solution)/shard_map/ppermute | solution.py:389
  34.4 16.1 %collective-permute-start.5 = (f32[8,64,512]{2,1,0:T(8,128)S(1)}, f32[8,64,512]{2,1,0:T(8,128)S(1)}, u32[]{:S(2)}, u32[]{:S(2)}) collective-permute-start(f32[8,64,512]{2,1,0:T(8,128)S(1)} %get-tuple-element.15), channel_id=1, source_target_pairs={{1,0},{2,1},{3,2},{4,3},{5,4},{6,5},{7,6},{8,7},{9,8},{10,9},{11,1... | collective-permute-start | bytes 3145736 | tf_op jit(solution)/shard_map/ppermute | solution.py:389
  129.5 1.5 %copy-start = (f32[8,10,64,128]{3,2,1,0:T(8,128)}, f32[8,10,64,128]{3,2,1,0:T(8,128)S(1)}, u32[]{:S(2)}) copy-start(f32[8,10,64,128]{3,2,1,0:T(8,128)S(1)} %get-tuple-element.12.refs_0_.refs_1_.refs_2_.refs_3_) | copy-start | bytes 7864324

commit v3 on v0

v3 whole, which is shorter than its diff:
```python
import functools

import jax
import jax.numpy as jnp
from jax import lax
from jax.experimental import pallas as pl
from jax.experimental.pallas import tpu as pltpu
from jax.sharding import PartitionSpec as P

B = 64
K = 6
G = 4
R = 32
H = 8
BB = B * B
GW = G * B
LANES = 128
WIDE = K // 2 * 3 * LANES
relaxation = 2.0 / 3.0
f32 = jnp.float32
bf16 = jnp.bfloat16


def lane_low(rows):
    return lax.broadcasted_iota(jnp.int32, (rows, LANES), 1) < B


def natural_dup(half_rows, scratch):
    low = lane_low(B // 2)
    swapped = pltpu.roll(half_rows, B, 1)
    scratch[pl.ds(0, B // 2, stride=2), :] = jnp.where(low, half_rows, swapped)
    scratch[pl.ds(1, B // 2, stride=2), :] = jnp.where(low, swapped, half_rows)


MESH = pl.DeviceIdType.MESH
PIECES = 5
ROWS = 4
CHUNK = ROWS * B


def split(value):
    high = value.astype(bf16)
    return high, (value - high.astype(f32)).astype(bf16)


def coarse_kernel(
    slots, columns, aggregate, owner, a_hbm, t_hbm, recv, got,
    a_tiles, t_tiles, t_nat, t_split, labels, codes, nat, smooth, aa, p_own,
    p_low, p_high, p_split, ap, own, below_out, above_out,
    lower_0, lower_1, lower_2, upper_0, upper_1, upper_2, label_rims, send,
    load_sem, rim_send, rim_recv, halo_send, halo_recv, near_send, near_recv, code_send, code_recv, row_send, row_recv, own_sem,
):
    me, row = lax.axis_index("col"), lax.axis_index("row")
    rows = lax.axis_size("row")
    device, count = row * slots + me, rows * slots

    def place(index):
        return (index // slots, lax.rem(index, slots))

    behind = place(lax.rem(device + count - 1, count))
    ahead = place(lax.rem(device + 1, count))
    lower, upper = (lower_0, lower_1, lower_2), (upper_0, upper_1, upper_2)
    core = lax.rem(me, 2)
    chip = me - core
    far, before, after = (lax.rem(chip + d, slots) for d in (4, 6, 2))
    peers = [far + core, far + 1 - core, after + core, before + core]
    peers += [after + 1 - core, before + 1 - core, chip + 1 - core]

    def load(source, target, index):
        copy = pltpu.make_async_copy(source, target, load_sem.at[index])
        copy.start()
        return copy

    half = pl.ds(0, B // 2)
    t_load = load(t_hbm, t_tiles.at[pl.ds(1, R // 8), half], 0)
    order = (1, 2, 0, 3)
    a_load = {tile: load(a_hbm.at[:, tile], a_tiles.at[tile, :, half], 1 + tile) for tile in order}
    for n in range(R):
        labels[n + H] = jnp.full((8, LANES), aggregate[n], jnp.int32)

    def here(target, i):
        return (lax.rem(lax.div(owner[i], G), slots) == target).astype(jnp.int32)

    for target in range(slots):
        code = sum(here(target, i) * (lax.rem(owner[i], G) + 1) for i in range(G))
        codes[target] = jnp.full((8, LANES), code, jnp.int32)
    barrier = pltpu.get_barrier_semaphore()
    targets = [(row, peer) for peer in peers] + [behind, ahead]
    for target in targets:
        pl.semaphore_signal(barrier, inc=1, device_id=target, device_id_type=MESH)
    pl.semaphore_wait(barrier, len(targets))

    def remote(source, target, here, there, where):
        copy = pltpu.make_async_remote_copy(
            src_ref=source, dst_ref=target, send_sem=here, recv_sem=there,
            device_id=where, device_id_type=MESH,
        )
        copy.start()
        return copy

    rims = [
        remote(t_hbm.at[R // 8 - 1], t_tiles.at[0, half], rim_send.at[0], rim_recv.at[0], ahead),
        remote(t_hbm.at[0], t_tiles.at[R // 8 + 1, half], rim_send.at[1], rim_recv.at[1], behind),
        remote(
            labels.at[pl.ds(R, H)], label_rims.at[0], rim_send.at[2], rim_recv.at[2], ahead
        ),
        remote(
            labels.at[pl.ds(H, H)], label_rims.at[1], rim_send.at[3], rim_recv.at[3],
            behind,
        ),
    ]
    copies = []
    for s, peer in enumerate(peers):
        copies.append(
            remote(codes.at[peer], got.at[me], code_send.at[s], code_recv.at[s], (row, peer))
        )
    has_low = (device > 0).astype(f32)
    has_high = (device < count - 1).astype(f32)

    low = lane_low(B)
    sub = lax.broadcasted_iota(jnp.int32, (B, LANES), 0)
    lane = lax.broadcasted_iota(jnp.int32, (B, LANES), 1)
    on_diagonal = sub == lane
    second = (lax.broadcasted_iota(jnp.int32, (8, LANES), 1) >= B).astype(jnp.int32)

    def split_basis(chunk):
        tiles = t_tiles.at[chunk].reshape((B // 2 + 1) * 8, LANES)

        def one(j, carry):
            n = chunk * 8 + j
            natural_dup(tiles[pl.ds(j, B // 2, stride=8), :], t_nat.at[n])
            high, rest = split(t_nat[n, 0:B, :])
            t_split[n, 0:B, :] = high
            t_split[n, B : 2 * B, :] = rest
            return carry

        lax.fori_loop(0, 8, one, 0)

    def column(n, k):
        return jnp.clip(columns[k, n] - device * R + H, 0, R + 2 * H - 1)

    def smooth_rows(tile):
        def one(r, carry):
            n = tile * 8 + r
            scale, previous, masks = None, None, []
            for k in range(K):
                ci = column(n, k)
                tiles = a_tiles.at[tile, k].reshape((B // 2 + 1) * 8, LANES)
                natural_dup(tiles[pl.ds(r, B // 2, stride=8), :], nat.at[k])
                value = nat[k, 0:B, :]
                if k == 0:
                    diagonal = jnp.sum(jnp.where(on_diagonal, value, 0.0), axis=1, keepdims=True)
                    scale = relaxation / diagonal
                high = value.astype(bf16).astype(f32)
                pieces = jnp.where(low, high, value - high).astype(bf16)
                base = (k // 2) * 3 * LANES
                aa[n, :, base + (k % 2) * LANES : base + (k % 2 + 1) * LANES] = pieces
                if k % 2 == 1:
                    both = jnp.where(low, previous, high).astype(bf16)
                    aa[n, :, base + 2 * LANES : base + 3 * LANES] = both
                previous = high
                basis = t_split[ci]
                weights = jnp.concatenate([basis[:B], basis[:B], basis[B:], basis[B:]], axis=0)
                applied = jnp.dot(
                    jnp.concatenate([pieces, pieces], axis=1), weights, preferred_element_type=f32
                )
                result = -applied * scale
                if k == 0:
                    result = result + t_nat[n + H, 0:B, :]
                smooth[k] = result.reshape(B // 8, 8, LANES)
                outside = jnp.logical_or(ci < H, ci >= R + H).astype(jnp.int32)
                masks.append(labels[ci] + outside * G)
            for part in range(4):
                total = None
                for k in range(K):
                    keep = masks[k] == 2 * part + second
                    term = jnp.where(keep[None], smooth[k], 0.0)
                    total = term if total is None else total + term
                p_own[n, :, part * LANES : (part + 1) * LANES] = total.reshape(B, LANES)
            return carry

        lax.fori_loop(0, 8, one, 0)

    t_load.wait()
    for chunk in range(1, R // 8 + 1):
        split_basis(chunk)
    for tile in (1, 2):
        a_load[tile].wait()
        smooth_rows(tile)
    for copy in rims:
        copy.wait_recv()
    labels[0:H] = label_rims[0]
    labels[R + H : R + 2 * H] = label_rims[1]
    split_basis(0)
    split_basis(R // 8 + 1)
    for tile in (0, 3):
        a_load[tile].wait()
        smooth_rows(tile)
    halo = [
        remote(p_own.at[pl.ds(R - H, H)], p_low, halo_send.at[0], halo_recv.at[0], ahead),
        remote(p_own.at[pl.ds(0, H)], p_high, halo_send.at[1], halo_recv.at[1], behind),
    ]

    def split_own(n, carry):
        high, low = split(p_own[n])
        p_split[n + H, 0:B, :] = high
        p_split[n + H, B : 2 * B, :] = low
        return carry

    lax.fori_loop(0, R, split_own, 0)
    own[...] = jnp.zeros_like(own)

    def applied_rows(chunk, slot):
        for r in range(ROWS):
            n = chunk * ROWS + r
            weights, marks = [], []
            for pair in range(K // 2):
                index = [column(n, 2 * pair + t) for t in range(2)]
                basis = [p_split[ci] for ci in index]
                side = [(ci < R // 2).astype(f32) for ci in index]
                for t in range(2):
                    marks.append(jnp.full((B, LANES), side[t], f32))
                    weights.extend([basis[t][:B], basis[t][:B]])
                marks.append(jnp.where(lane_low(B), side[0], side[1]))
                weights.extend([basis[0][B:], basis[1][B:]])
            left = aa[n]
            marks = jnp.concatenate(marks, axis=1).astype(bf16)
            weights = jnp.concatenate(weights, axis=0)
            below = left * marks
            middle = jnp.dot(left, weights[:, :GW], preferred_element_type=f32)
            sides = jnp.dot(
                jnp.concatenate([below, left - below], axis=0),
                weights[:, GW:],
                preferred_element_type=f32,
            )
            for g, value in enumerate((sides[:B], middle, sides[B:])):
                high, low = split(value)
                ap[slot, 0, r * B : (r + 1) * B, g * GW : (g + 1) * GW] = high
                ap[slot, 1, r * B : (r + 1) * B, g * GW : (g + 1) * GW] = low

    def turned(chunk, part):
        block = p_own[pl.ds(chunk * ROWS, ROWS), :, part * GW : (part + 1) * GW]
        return split(block.reshape(CHUNK, GW).T)

    def product(left, slot, lanes):
        high, low = left
        value = jnp.dot(high, ap[slot, 0, :, lanes], preferred_element_type=f32)
        value = value + jnp.dot(low, ap[slot, 0, :, lanes], preferred_element_type=f32)
        return value + jnp.dot(high, ap[slot, 1, :, lanes], preferred_element_type=f32)

    def add_own(chunk, slot):
        value = product(turned(chunk, 0), slot, slice(0, 3 * GW))
        for t in range(6):
            tile = value[:, t * LANES : (t + 1) * LANES].reshape(G, B, LANES)
            own[t // 2, :, t % 2] += tile

    def inner(chunk, carry):
        applied_rows(chunk, 0)
        add_own(chunk, 0)
        return carry

    lax.fori_loop(H // ROWS, (R - H) // ROWS, inner, 0)

    for copy in halo:
        copy.wait_recv()
    for source, base in ((p_low, 0), (p_high, R + H)):

        def split_halo(n, carry, source=source, base=base):
            for half in range(2):
                high, low = split(source[n, :, (1 - half) * GW : (2 - half) * GW])
                p_split[base + n, 0:B, half * GW : (half + 1) * GW] = high
                p_split[base + n, B : 2 * B, half * GW : (half + 1) * GW] = low
            return carry

        lax.fori_loop(0, H, split_halo, 0)

    def rim_chunk(index):
        return index + (index // 2) * 4

    def rim(index, carry):
        applied_rows(rim_chunk(index), index)
        return carry

    lax.fori_loop(0, 4, rim, 0)

    left_below = [turned(rim_chunk(index), 1) for index in (0, 1)]
    left_above = [turned(rim_chunk(index), 1) for index in (2, 3)]
    near = {}
    for turn in range(3):
        for side, lefts, out, landing, g, base, where in (
            (0, left_above, above_out, lower, turn, 2, ahead),
            (1, left_below, below_out, upper, 2 - turn, 0, behind),
        ):
            lanes = slice(g * GW, (g + 1) * GW)
            value = product(lefts[0], base, lanes) + product(lefts[1], base + 1, lanes)
            for half in range(2):
                tile = value[:, half * LANES : (half + 1) * LANES].reshape(G, B, LANES)
                out[g, :, half] = tile
            near[side, g] = remote(
                out.at[g], landing[g], near_send.at[side, g], near_recv.at[side, g], where
            )
    for index in range(4):
        add_own(rim_chunk(index), index)

    def build(target, piece):
        a = functools.reduce(jnp.maximum, [here(target, i) * i for i in range(1, G)])
        for half in range(2):
            terms = []
            if piece < 3:
                terms.append(lower[piece][a, half] * has_low)
            if 1 <= piece < 4:
                terms.append(own[piece - 1, a, half])
            if piece >= 2:
                terms.append(upper[piece - 2][a, half] * has_high)
            send[target, piece, half] = functools.reduce(jnp.add, terms)

    needs = {0: [(0, 0)], 4: [(1, 2)], 1: [(0, 1)], 3: [(1, 1)], 2: [(0, 2), (1, 0)]}
    for piece in (0, 4, 1, 3, 2):
        for key in needs[piece]:
            near[key].wait_recv()
        for s, peer in enumerate(peers):
            build(peer, piece)
            copies.append(
                remote(
                    send.at[peer, piece], recv.at[me, piece],
                    row_send.at[piece, s], row_recv.at[piece, s], (row, peer),
                )
            )
        build(me, piece)
    for index, (source, target) in enumerate(((codes, got), (send, recv))):
        copy = pltpu.make_async_copy(source.at[me], target.at[me], own_sem.at[index])
        copy.start()
        copies.append(copy)
    for copy in rims + halo + list(near.values()):
        copy.wait_send()
    for copy in copies:
        copy.wait()


def coarse_rows(columns, aggregate, owner, a_blocks, tentative, slots):
    anywhere = pl.BlockSpec(memory_space=pl.ANY)
    vmem = pl.BlockSpec(memory_space=pltpu.VMEM)
    smem = pl.BlockSpec(memory_space=pltpu.SMEM)
    dma = pltpu.SemaphoreType.DMA
    part = pltpu.VMEM((3, G, 2, B, LANES), f32)
    piece = pltpu.VMEM((G, 2, B, LANES), f32)
    a_tiled = a_blocks.reshape(R // 8, 8, K, B // 2, LANES).transpose(2, 0, 3, 1, 4)
    t_tiled = tentative.reshape(R // 8, 8, B // 2, LANES).transpose(0, 2, 1, 3)
    return pl.pallas_call(
        functools.partial(coarse_kernel, slots),
        out_shape=(
            jax.ShapeDtypeStruct((slots, PIECES, 2, B, LANES), f32),
            jax.ShapeDtypeStruct((slots, 8, LANES), jnp.int32),
        ),
        in_specs=[smem, smem, smem, anywhere, anywhere],
        out_specs=(anywhere, vmem),
        scratch_shapes=[
            pltpu.VMEM((R // 8, K, B // 2 + 1, 8, LANES), f32),
            pltpu.VMEM((R // 8 + 2, B // 2 + 1, 8, LANES), f32),
            pltpu.VMEM((R + 2 * H, B + 8, LANES), f32),
            pltpu.VMEM((R + 2 * H, 2 * B, LANES), bf16),
            pltpu.VMEM((R + 2 * H, 8, LANES), jnp.int32),
            pltpu.VMEM((slots, 8, LANES), jnp.int32),
            pltpu.VMEM((K, B + 8, LANES), f32),
            pltpu.VMEM((K, B // 8, 8, LANES), f32),
            pltpu.VMEM((R, B, WIDE), bf16),
            pltpu.VMEM((R, B, 2 * GW), f32),
            pltpu.VMEM((H, B, 2 * GW), f32),
            pltpu.VMEM((H, B, 2 * GW), f32),
            pltpu.VMEM((R + 2 * H, 2 * B, 2 * GW), bf16),
            pltpu.VMEM((4, 2, CHUNK, 3 * GW), bf16),
            part, part, part,
            piece, piece, piece, piece, piece, piece,
            pltpu.VMEM((2, H, 8, LANES), jnp.int32),
            pltpu.VMEM((slots, PIECES, 2, B, LANES), f32),
            dma((1 + R // 8,)),
            dma((4,)), dma((4,)),
            dma((2,)), dma((2,)),
            dma((2, 3)), dma((2, 3)),
            dma((slots,)), dma((slots,)),
            dma((PIECES, slots)), dma((PIECES, slots)),
            dma((2,)),
        ],
        compiler_params=pltpu.CompilerParams(
            collective_id=0, has_side_effects=True, vmem_limit_bytes=48 << 20
        ),
        name="coarse",
    )(columns.T, aggregate, owner, a_tiled, t_tiled)


def final_kernel(source, *refs):
    blocks, out_ref, pairs = refs[:G], refs[G], refs[G + 1]
    low = lane_low(B // 2)
    tiles = 2
    for g in range(G):
        for j in range(tiles):
            even = blocks[g][0, 0, j, pl.ds(0, B // 2, stride=2), :]
            odd = blocks[g][0, 0, j, pl.ds(1, B // 2, stride=2), :]
            base = (g * tiles + j) * B
            pairs[pl.ds(base, B // 2), :] = jnp.where(low, even, pltpu.roll(odd, B, 1))
            pairs[pl.ds(base + B // 2, B // 2), :] = jnp.where(low, pltpu.roll(even, B, 1), odd)
    for col in range(2 * tiles):
        for c in range(B // 2):
            rows = pl.ds(col * (B // 2) + c, G, stride=tiles * B)
            out_ref[col, :, c * LANES : (c + 1) * LANES] = pairs[rows, :]


def final(recv, source):
    tiles = 2
    specs = [
        pl.BlockSpec((1, 1, tiles, B, LANES), lambda j, source, g=g: (source[g], j, 0, 0, 0))
        for g in range(G)
    ]
    result = pl.pallas_call(
        final_kernel,
        out_shape=jax.ShapeDtypeStruct((5 * G, G, BB), f32),
        grid_spec=pltpu.PrefetchScalarGridSpec(
            num_scalar_prefetch=1,
            grid=(PIECES,),
            in_specs=specs,
            out_specs=pl.BlockSpec((2 * tiles, G, BB), lambda j, source: (j, 0, 0)),
            scratch_shapes=[pltpu.VMEM((2 * G * tiles * B, LANES), f32)],
        ),
        name="final",
    )(source, recv, recv, recv, recv)
    return result.transpose(1, 0, 2)


def local(a_blocks, columns, tentative, aggregate, owner):
    slots = lax.axis_size("col")
    recv, got = coarse_rows(columns, aggregate, owner, a_blocks, tentative, slots)
    places = got[:, 0, 0]
    wanted = places[None, :] == jnp.arange(1, G + 1, dtype=jnp.int32)[:, None]
    source = jnp.sum(wanted * jnp.arange(slots, dtype=jnp.int32)[None, :], axis=1)
    return final(recv, source.astype(jnp.int32))


def solution(mesh):
    placed = (
        P(("row", "col"), None, None),
        P(("row", "col"), None),
        P(("row", "col"), None),
        P(("row", "col")),
        P(("row", "col")),
    )
    return jax.shard_map(
        local, mesh=mesh, in_specs=placed, out_specs=P(("row", "col"), None, None), check_vma=False
    )
```

time: 739 us -> 92.3 us (0.12); the launches traced: 726 us -> 91 us
  local copies, waits for them, and re-layouts: 284 us -> 4.78 us
  matrix products: 233 us -> 0 us
  waiting for transfers between devices: 91.4 us -> 0 us
  Pallas kernels: 0 us -> 85.4 us
  other arithmetic: 56.1 us -> 0.77 us
  starting transfers between devices: 27.7 us -> 0 us
  blocking collectives: 18.5 us -> 0 us
  between operations: 14.6 us -> 0.02 us
    dot_general x29 -> x0, matrix products: 233 us -> none  [the longest x20 103 us: apply_rows(): jnp.einsum('sqp,scpw->scqw', a_mats[:, stored], gathered[:, stored], prec...]
    gather x19 -> x0, local copies, waits for them, and re-layouts: 211 us -> none  [the longest x12 192 us: apply_rows(): jnp.take(ext_dense, index_group, axis=0).reshape(count, K, 3 * G, B, BC)]
    pallas_call x0 -> x2, Pallas kernels: none -> 85.4 us  [the longest x1 80.1 us: coarse_rows(): pl.pallas_call(functools.partial(coarse_kernel, slots), out_shape=(jax.Sh...]
    all_gather x1 -> x0, waiting for transfers between devices: 68.9 us -> none  [local(): lax.all_gather(coarse_rows, 'col', axis=0, tiled=True)]
    select_n x9 -> x0, other arithmetic: 55.2 us -> none  [the longest x8 55.2 us: apply_rows(): jnp.take(ext_dense, index_group, axis=0).reshape(count, K, 3 * G, B, BC)]
    reshape x9 -> x0, local copies, waits for them, and re-layouts: 31.8 us -> none  [the longest x2 13.6 us: prolong_rows(): return (smooth.reshape(row_count, K, B * BC), labels)]
    ppermute x10 -> x0, starting transfers between devices: 27.7 us -> none  [the longest x4 14.3 us: padded(): lax.ppermute(lax.slice_in_dim(block, block.shape[dim] - width, None, axis...]
    ppermute x10 -> x0, waiting for transfers between devices: 22.4 us -> none  [the longest x2 19.6 us: from_behind(): return lax.ppermute(block, axis, route)]
  transfers between devices with their start and end apart: 11 -> 0, of which waited for: 4 -> 0; matrix products, arithmetic and copies ran while one was open for 7% -> 0% of each run, Pallas kernels for 0% -> 0%
where the time goes in v3:
time: 92.3 us; the launch traced here: 91 us
  Pallas kernels  85.4 us (93%)
  local copies, waits for them, and re-layouts  4.78 us (5%)
    pallas_call x1, Pallas kernels, coarse_rows(): pl.pallas_call(functools.partial(coarse_kernel, slots), out_shape=(jax.Sh...  80.1 us
    pallas_call x1, Pallas kernels, final(): pl.pallas_call(final_kernel, out_shape=jax.ShapeDtypeStruct((5 * G, G, BB...  5.34 us
    unnamed x10, local copies, waits for them, and re-layouts  4.55 us

profile of v3, /device:TPU:1, one launch (start us, length us, event | category | flops | bytes accessed | tf_op | source)
XLA Modules:
  0.0 91.0 jit_solution(4575214714285844674)
XLA Ops:
  0.0 0.0 copy-start.1
  0.0 1.0 %copy-done.1 = f32[32,4096]{1,0:T(8,128)S(1)} copy-done((f32[32,4096]{1,0:T(8,128)S(1)}, f32[32,4096]{1,0:T(8,128)}, u32[]{:S(2)}) %copy-start.1) | copy-done | bytes 524312
  1.0 0.0 copy-start.2
  1.0 0.7 copy-done.2
  1.7 0.0 copy-start.3
  1.7 0.7 copy-done.3
  2.4 0.0 copy-start.4
  2.4 0.7 copy-done.4
  3.0 80.1 %coarse.1 = (f32[8,5,2,64,128]{4,3,2,1,0:T(8,128)S(1)}, s32[8,8,128]{2,1,0:T(8,128)S(1)}) custom-call(s32[6,32]{1,0:T(8,128)S(1)} %bitcast.9, s32[32]{0:T(128)S(1)} %copy-done.3, s32[4]{0:T(128)S(1)} %copy-done.4, f32[6,4,32,8,128]{4,3,2,1,0:T(8,128)} %bitcast.10, f32[4,32,8,128]{3,2,1,0:T(8,128)S(1)} %bitcast.8), custom_call_target="tpu_custom_call" | custom-call | tf_op jit(solution)/shard_map/coarse/pallas_call | solution.py:349
  83.1 0.0 copy-start
  83.1 1.5 %copy-done = f32[8,5,2,64,128]{4,3,2,1,0:T(8,128)} copy-done((f32[8,5,2,64,128]{4,3,2,1,0:T(8,128)}, f32[8,5,2,64,128]{4,3,2,1,0:T(8,128)S(1)}, u32[]{:S(2)}) %copy-start) | copy-done | bytes 2621464
  84.6 0.2 slice_reduce_fusion
  84.9 0.8 select_reduce_fusion.source
  85.6 5.3 %final.1 = f32[20,4,4096]{2,1,0:T(4,128)} custom-call(s32[4]{0:T(128)} %select_reduce_fusion.source, f32[8,5,2,64,128]{4,3,2,1,0:T(8,128)} %copy-done, f32[8,5,2,64,128]{4,3,2,1,0:T(8,128)} %copy-done, f32[8,5,2,64,128]{4,3,2,1,0:T(8,128)} %copy-done, f32[8,5,2,64,128]{4,3,2,1,0:T(8,128)} %copy-done), custom_call_target="tpu_custom_call" | custom-call | tf_op jit(solution)/shard_map/final/pallas_call | solution.py:414
  (1 shorter events, 0.0 us)
Async XLA Ops:
  0.0 1.0 %copy-start.1 = (f32[32,4096]{1,0:T(8,128)S(1)}, f32[32,4096]{1,0:T(8,128)}, u32[]{:S(2)}) copy-start(f32[32,4096]{1,0:T(8,128)} %param.7) | copy-start | bytes 1572868
  1.0 0.7 copy-start.2
  1.7 0.7 copy-start.3
  2.4 0.7 copy-start.4
  83.1 1.5 %copy-start = (f32[8,5,2,64,128]{4,3,2,1,0:T(8,128)}, f32[8,5,2,64,128]{4,3,2,1,0:T(8,128)S(1)}, u32[]{:S(2)}) copy-start(f32[8,5,2,64,128]{4,3,2,1,0:T(8,128)S(1)} %get-tuple-element.8.refs_0_.refs_1_.refs_2_.refs_3_) | copy-start | bytes 7864324

commit v4 on v3

--- a/solution.py
+++ b/solution.py
@@ -44,11 +44,11 @@
 
 
 def coarse_kernel(
-    slots, columns, aggregate, owner, a_hbm, t_hbm, recv, got,
+    slots, columns, aggregate, owner, a_hbm, t_hbm, out_ref,
     a_tiles, t_tiles, t_nat, t_split, labels, codes, nat, smooth, aa, p_own,
     p_low, p_high, p_split, ap, own, below_out, above_out,
-    lower_0, lower_1, lower_2, upper_0, upper_1, upper_2, label_rims, send,
-    load_sem, rim_send, rim_recv, halo_send, halo_recv, near_send, near_recv, code_send, code_recv, row_send, row_recv, own_sem,
+    lower_0, lower_1, lower_2, upper_0, upper_1, upper_2, label_rims, send, recv, got, chosen, pairs,
+    load_sem, rim_send, rim_recv, halo_send, halo_recv, near_send, near_recv, code_send, code_recv, row_send, row_recv,
 ):
     me, row = lax.axis_index("col"), lax.axis_index("row")
     rows = lax.axis_size("row")
@@ -73,7 +73,7 @@
 
     half = pl.ds(0, B // 2)
     t_load = load(t_hbm, t_tiles.at[pl.ds(1, R // 8), half], 0)
-    order = (1, 2, 0, 3)
+    order = (1, 0, 3, 2)
     a_load = {tile: load(a_hbm.at[:, tile], a_tiles.at[tile, :, half], 1 + tile) for tile in order}
     for n in range(R):
         labels[n + H] = jnp.full((8, LANES), aggregate[n], jnp.int32)
@@ -184,22 +184,25 @@
     t_load.wait()
     for chunk in range(1, R // 8 + 1):
         split_basis(chunk)
-    for tile in (1, 2):
+    def smooth_tile(tile):
         a_load[tile].wait()
         smooth_rows(tile)
+
+    smooth_tile(1)
     for copy in rims:
         copy.wait_recv()
     labels[0:H] = label_rims[0]
     labels[R + H : R + 2 * H] = label_rims[1]
     split_basis(0)
+    smooth_tile(0)
+    halo_low = remote(p_own.at[pl.ds(0, H)], p_high, halo_send.at[1], halo_recv.at[1], behind)
     split_basis(R // 8 + 1)
-    for tile in (0, 3):
-        a_load[tile].wait()
-        smooth_rows(tile)
-    halo = [
-        remote(p_own.at[pl.ds(R - H, H)], p_low, halo_send.at[0], halo_recv.at[0], ahead),
-        remote(p_own.at[pl.ds(0, H)], p_high, halo_send.at[1], halo_recv.at[1], behind),
-    ]
+    smooth_tile(3)
+    halo_high = remote(
+        p_own.at[pl.ds(R - H, H)], p_low, halo_send.at[0], halo_recv.at[0], ahead
+    )
+    smooth_tile(2)
+    halo = [halo_low, halo_high]
 
     def split_own(n, carry):
         high, low = split(p_own[n])
@@ -274,33 +277,32 @@
 
         lax.fori_loop(0, H, split_halo, 0)
 
-    def rim_chunk(index):
-        return index + (index // 2) * 4
-
-    def rim(index, carry):
-        applied_rows(rim_chunk(index), index)
-        return carry
-
-    lax.fori_loop(0, 4, rim, 0)
-
-    left_below = [turned(rim_chunk(index), 1) for index in (0, 1)]
-    left_above = [turned(rim_chunk(index), 1) for index in (2, 3)]
     near = {}
-    for turn in range(3):
-        for side, lefts, out, landing, g, base, where in (
-            (0, left_above, above_out, lower, turn, 2, ahead),
-            (1, left_below, below_out, upper, 2 - turn, 0, behind),
-        ):
+
+    def rim(first, side, out, landing, turns, where):
+        def one(index, carry):
+            applied_rows(first + index, 2 * side + index)
+            return carry
+
+        lax.fori_loop(0, 2, one, 0)
+        lefts = [turned(first + index, 1) for index in range(2)]
+        for g in turns:
             lanes = slice(g * GW, (g + 1) * GW)
-            value = product(lefts[0], base, lanes) + product(lefts[1], base + 1, lanes)
+            value = product(lefts[0], 2 * side, lanes) + product(lefts[1], 2 * side + 1, lanes)
             for half in range(2):
                 tile = value[:, half * LANES : (half + 1) * LANES].reshape(G, B, LANES)
                 out[g, :, half] = tile
             near[side, g] = remote(
                 out.at[g], landing[g], near_send.at[side, g], near_recv.at[side, g], where
             )
-    for index in range(4):
-        add_own(rim_chunk(index), index)
+
+    rim((R - H) // ROWS, 0, above_out, lower, (0, 1, 2), ahead)
+    rim(0, 1, below_out, upper, (2, 1, 0), behind)
+
+    def sum_own():
+        for index in range(2):
+            add_own((R - H) // ROWS + index, index)
+            add_own(index, 2 + index)
 
     def build(target, piece):
         a = functools.reduce(jnp.maximum, [here(target, i) * i for i in range(1, G)])
@@ -315,26 +317,68 @@
             send[target, piece, half] = functools.reduce(jnp.add, terms)
 
     needs = {0: [(0, 0)], 4: [(1, 2)], 1: [(0, 1)], 3: [(1, 1)], 2: [(0, 2), (1, 0)]}
-    for piece in (0, 4, 1, 3, 2):
+    pieces_order = (0, 4, 1, 3, 2)
+    arrivals = {}
+    for step, piece in enumerate(pieces_order):
+        if step == 1:
+            sum_own()
         for key in needs[piece]:
             near[key].wait_recv()
+        arrivals[piece] = []
         for s, peer in enumerate(peers):
             build(peer, piece)
-            copies.append(
+            arrivals[piece].append(
                 remote(
                     send.at[peer, piece], recv.at[me, piece],
                     row_send.at[piece, s], row_recv.at[piece, s], (row, peer),
                 )
             )
         build(me, piece)
-    for index, (source, target) in enumerate(((codes, got), (send, recv))):
-        copy = pltpu.make_async_copy(source.at[me], target.at[me], own_sem.at[index])
-        copy.start()
-        copies.append(copy)
-    for copy in rims + halo + list(near.values()):
+
+    for copy in copies:
+        copy.wait_recv()
+    half_low = lane_low(B // 2)
+    for piece in pieces_order:
+        for copy in arrivals[piece]:
+            copy.wait_recv()
+        for half in range(2):
+            totals = [None] * G
+            for index in range(slots):
+                if index == slots - 1:
+                    code, block = codes[me], send[me, piece, half]
+                else:
+                    code, block = got[peers[index]], recv[peers[index], piece, half]
+                block = block.reshape(B // 8, 8, LANES)
+                for g in range(G):
+                    term = jnp.where((code == g + 1)[None], block, 0.0)
+                    totals[g] = term if totals[g] is None else totals[g] + term
+            for g in range(G):
+                chosen[g, half, 0:B, :] = totals[g].reshape(B, LANES)
+        for g in range(G):
+            for half in range(2):
+                even = chosen[g, half, pl.ds(0, B // 2, stride=2), :]
+                odd = chosen[g, half, pl.ds(1, B // 2, stride=2), :]
+                base = (g * 2 + half) * B
+                pairs[base : base + B // 2, :] = jnp.where(
+                    half_low, even, pltpu.roll(odd, B, 1)
+                )
+                pairs[base + B // 2 : base + B, :] = jnp.where(
+                    half_low, pltpu.roll(even, B, 1), odd
+                )
+
+        def write(c, carry, piece=piece):
+            lanes = pl.ds(pl.multiple_of(c * LANES, LANES), LANES)
+            for col in range(4):
+                rows_of = pl.ds(col * (B // 2) + c, G, stride=2 * B)
+                out_ref[piece * 4 + col, :, lanes] = pairs[rows_of, :]
+            return carry
+
+        lax.fori_loop(0, B // 2, write, 0, unroll=4)
+    for copy in rims + halo + list(near.values()) + copies:
         copy.wait_send()
-    for copy in copies:
-        copy.wait()
+    for piece in pieces_order:
+        for copy in arrivals[piece]:
+            copy.wait_send()
 
 
 def coarse_rows(columns, aggregate, owner, a_blocks, tentative, slots):
@@ -348,12 +392,9 @@
     t_tiled = tentative.reshape(R // 8, 8, B // 2, LANES).transpose(0, 2, 1, 3)
     return pl.pallas_call(
         functools.partial(coarse_kernel, slots),
-        out_shape=(
-            jax.ShapeDtypeStruct((slots, PIECES, 2, B, LANES), f32),
-            jax.ShapeDtypeStruct((slots, 8, LANES), jnp.int32),
-        ),
+        out_shape=jax.ShapeDtypeStruct((5 * G, G, BB), f32),
         in_specs=[smem, smem, smem, anywhere, anywhere],
-        out_specs=(anywhere, vmem),
+        out_specs=vmem,
         scratch_shapes=[
             pltpu.VMEM((R // 8, K, B // 2 + 1, 8, LANES), f32),
             pltpu.VMEM((R // 8 + 2, B // 2 + 1, 8, LANES), f32),
@@ -373,13 +414,16 @@
             piece, piece, piece, piece, piece, piece,
             pltpu.VMEM((2, H, 8, LANES), jnp.int32),
             pltpu.VMEM((slots, PIECES, 2, B, LANES), f32),
+            pltpu.VMEM((slots, PIECES, 2, B, LANES), f32),
+            pltpu.VMEM((slots, 8, LANES), jnp.int32),
+            pltpu.VMEM((G, 2, B + 8, LANES), f32),
+            pltpu.VMEM((4 * G * B, LANES), f32),
             dma((1 + R // 8,)),
             dma((4,)), dma((4,)),
             dma((2,)), dma((2,)),
             dma((2, 3)), dma((2, 3)),
             dma((slots,)), dma((slots,)),
             dma((PIECES, slots)), dma((PIECES, slots)),
-            dma((2,)),
         ],
         compiler_params=pltpu.CompilerParams(
             collective_id=0, has_side_effects=True, vmem_limit_bytes=48 << 20
@@ -388,51 +432,10 @@
     )(columns.T, aggregate, owner, a_tiled, t_tiled)
 
 
-def final_kernel(source, *refs):
-    blocks, out_ref, pairs = refs[:G], refs[G], refs[G + 1]
-    low = lane_low(B // 2)
-    tiles = 2
-    for g in range(G):
-        for j in range(tiles):
-            even = blocks[g][0, 0, j, pl.ds(0, B // 2, stride=2), :]
-            odd = blocks[g][0, 0, j, pl.ds(1, B // 2, stride=2), :]
-            base = (g * tiles + j) * B
-            pairs[pl.ds(base, B // 2), :] = jnp.where(low, even, pltpu.roll(odd, B, 1))
-            pairs[pl.ds(base + B // 2, B // 2), :] = jnp.where(low, pltpu.roll(even, B, 1), odd)
-    for col in range(2 * tiles):
-        for c in range(B // 2):
-            rows = pl.ds(col * (B // 2) + c, G, stride=tiles * B)
-            out_ref[col, :, c * LANES : (c + 1) * LANES] = pairs[rows, :]
-
-
-def final(recv, source):
-    tiles = 2
-    specs = [
-        pl.BlockSpec((1, 1, tiles, B, LANES), lambda j, source, g=g: (source[g], j, 0, 0, 0))
-        for g in range(G)
-    ]
-    result = pl.pallas_call(
-        final_kernel,
-        out_shape=jax.ShapeDtypeStruct((5 * G, G, BB), f32),
-        grid_spec=pltpu.PrefetchScalarGridSpec(
-            num_scalar_prefetch=1,
-            grid=(PIECES,),
-            in_specs=specs,
-            out_specs=pl.BlockSpec((2 * tiles, G, BB), lambda j, source: (j, 0, 0)),
-            scratch_shapes=[pltpu.VMEM((2 * G * tiles * B, LANES), f32)],
-        ),
-        name="final",
-    )(source, recv, recv, recv, recv)
-    return result.transpose(1, 0, 2)
-
-
 def local(a_blocks, columns, tentative, aggregate, owner):
     slots = lax.axis_size("col")
-    recv, got = coarse_rows(columns, aggregate, owner, a_blocks, tentative, slots)
-    places = got[:, 0, 0]
-    wanted = places[None, :] == jnp.arange(1, G + 1, dtype=jnp.int32)[:, None]
-    source = jnp.sum(wanted * jnp.arange(slots, dtype=jnp.int32)[None, :], axis=1)
-    return final(recv, source.astype(jnp.int32))
+    result = coarse_rows(columns, aggregate, owner, a_blocks, tentative, slots)
+    return result.transpose(1, 0, 2)
 
 
 def solution(mesh):

time: 92.3 us -> 86.4 us (0.936)
  Pallas kernels: 85.4 us -> 79.7 us
  local copies, waits for them, and re-layouts: 4.78 us -> 5.98 us
    pallas_call x2 -> x1, Pallas kernels: 85.4 us -> 79.7 us  [coarse_rows(): pl.pallas_call(functools.partial(coarse_kernel, slots), out_shape=jax.Sha...]
    unnamed x10 -> x11, local copies, waits for them, and re-layouts: 4.55 us -> 5.98 us
where the time goes in v4:
time: 86.4 us; the launch traced here: 85.7 us
  Pallas kernels  79.7 us (92%)
  local copies, waits for them, and re-layouts  5.98 us (7%)
    pallas_call x1, Pallas kernels, coarse_rows(): pl.pallas_call(functools.partial(coarse_kernel, slots), out_shape=jax.Sha...  79.7 us
    unnamed x11, local copies, waits for them, and re-layouts  5.98 us

profile of v4, /device:TPU:1, one launch (start us, length us, event | category | flops | bytes accessed | tf_op | source)
XLA Modules:
  0.0 85.7 jit_solution(6194647604203896744)
XLA Ops:
  0.0 0.0 copy-start
  0.0 1.9 %copy-done = f32[32,6,4096]{2,0,1:T(8,128)S(1)} copy-done((f32[32,6,4096]{2,0,1:T(8,128)S(1)}, f32[32,6,4096]{2,0,1:T(8,128)}, u32[]{:S(2)}) %copy-start) | copy-done | bytes 3145752
  1.9 0.0 copy-start.1
  1.9 1.0 %copy-done.1 = f32[32,4096]{1,0:T(8,128)S(1)} copy-done((f32[32,4096]{1,0:T(8,128)S(1)}, f32[32,4096]{1,0:T(8,128)}, u32[]{:S(2)}) %copy-start.1) | copy-done | bytes 524312
  2.9 0.0 copy-start.2
  2.9 0.7 copy-done.2
  3.6 0.0 copy-start.3
  3.6 0.7 copy-done.3
  4.3 0.0 copy-start.4
  4.3 0.7 copy-done.4
  4.9 79.7 %coarse.1 = f32[20,4,4096]{2,1,0:T(4,128)S(1)} custom-call(s32[6,32]{1,0:T(8,128)S(1)} %bitcast.11, s32[32]{0:T(128)S(1)} %copy-done.3, s32[4]{0:T(128)S(1)} %copy-done.4, f32[6,4,32,8,128]{4,3,2,1,0:T(8,128)S(1)} %bitcast.9, f32[4,32,8,128]{3,2,1,0:T(8,128)S(1)} %bitcast.10), custom_call_target="tpu_custom_call" | custom-call | tf_op jit(solution)/shard_map/coarse/pallas_call | solution.py:393
  84.7 1.1 %copy.7 = f32[4,20,4096]{2,0,1:T(4,128)} copy(f32[4,20,4096]{2,0,1:T(4,128)S(1)} %bitcast.8) | data formatting | bytes 2621440
Async XLA Ops:
  0.0 1.9 %copy-start = (f32[32,6,4096]{2,0,1:T(8,128)S(1)}, f32[32,6,4096]{2,0,1:T(8,128)}, u32[]{:S(2)}) copy-start(f32[32,6,4096]{2,0,1:T(8,128)} %param.5) | copy-start | bytes 9437188
  1.9 1.0 %copy-start.1 = (f32[32,4096]{1,0:T(8,128)S(1)}, f32[32,4096]{1,0:T(8,128)}, u32[]{:S(2)}) copy-start(f32[32,4096]{1,0:T(8,128)} %param.7) | copy-start | bytes 1572868
  2.9 0.7 copy-start.2
  3.6 0.7 copy-start.3
  4.3 0.7 copy-start.4

commit v5 on v4

--- a/solution.py
+++ b/solution.py
@@ -73,7 +73,7 @@
 
     half = pl.ds(0, B // 2)
     t_load = load(t_hbm, t_tiles.at[pl.ds(1, R // 8), half], 0)
-    order = (1, 0, 3, 2)
+    order = (0, 3, 1, 2)
     a_load = {tile: load(a_hbm.at[:, tile], a_tiles.at[tile, :, half], 1 + tile) for tile in order}
     for n in range(R):
         labels[n + H] = jnp.full((8, LANES), aggregate[n], jnp.int32)
@@ -134,12 +134,12 @@
             t_split[n, B : 2 * B, :] = rest
             return carry
 
-        lax.fori_loop(0, 8, one, 0)
+        lax.fori_loop(0, 8, one, 0, unroll=4)
 
     def column(n, k):
         return jnp.clip(columns[k, n] - device * R + H, 0, R + 2 * H - 1)
 
-    def smooth_rows(tile):
+    def smooth_rows(tile, first=0, count=8):
         def one(r, carry):
             n = tile * 8 + r
             scale, previous, masks = None, None, []
@@ -179,30 +179,40 @@
                 p_own[n, :, part * LANES : (part + 1) * LANES] = total.reshape(B, LANES)
             return carry
 
-        lax.fori_loop(0, 8, one, 0)
+        lax.fori_loop(first, first + count, one, 0, unroll=2)
 
     t_load.wait()
     for chunk in range(1, R // 8 + 1):
         split_basis(chunk)
-    def smooth_tile(tile):
-        a_load[tile].wait()
-        smooth_rows(tile)
-
-    smooth_tile(1)
     for copy in rims:
         copy.wait_recv()
     labels[0:H] = label_rims[0]
     labels[R + H : R + 2 * H] = label_rims[1]
     split_basis(0)
-    smooth_tile(0)
-    halo_low = remote(p_own.at[pl.ds(0, H)], p_high, halo_send.at[1], halo_recv.at[1], behind)
     split_basis(R // 8 + 1)
-    smooth_tile(3)
-    halo_high = remote(
-        p_own.at[pl.ds(R - H, H)], p_low, halo_send.at[0], halo_recv.at[0], ahead
-    )
-    smooth_tile(2)
-    halo = [halo_low, halo_high]
+    a_load[0].wait()
+    a_load[3].wait()
+    halo_from_ahead, halo_from_behind = [], []
+    for part in range(2):
+        window = pl.ds(part * ROWS, ROWS)
+        smooth_rows(0, part * ROWS, ROWS)
+        halo_from_ahead.append(
+            remote(
+                p_own.at[window], p_high.at[window], halo_send.at[1, part],
+                halo_recv.at[1, part], behind,
+            )
+        )
+        smooth_rows(3, part * ROWS, ROWS)
+        halo_from_behind.append(
+            remote(
+                p_own.at[pl.ds(R - H + part * ROWS, ROWS)], p_low.at[window],
+                halo_send.at[0, part], halo_recv.at[0, part], ahead,
+            )
+        )
+    for tile in (1, 2):
+        a_load[tile].wait()
+        smooth_rows(tile)
+    halo = halo_from_ahead + halo_from_behind
 
     def split_own(n, carry):
         high, low = split(p_own[n])
@@ -210,7 +220,7 @@
         p_split[n + H, B : 2 * B, :] = low
         return carry
 
-    lax.fori_loop(0, R, split_own, 0)
+    lax.fori_loop(0, R, split_own, 0, unroll=2)
     own[...] = jnp.zeros_like(own)
 
     def applied_rows(chunk, slot):
@@ -258,24 +268,23 @@
             own[t // 2, :, t % 2] += tile
 
     def inner(chunk, carry):
-        applied_rows(chunk, 0)
-        add_own(chunk, 0)
+        applied_rows(chunk, chunk + 2)
         return carry
 
     lax.fori_loop(H // ROWS, (R - H) // ROWS, inner, 0)
 
-    for copy in halo:
-        copy.wait_recv()
-    for source, base in ((p_low, 0), (p_high, R + H)):
-
-        def split_halo(n, carry, source=source, base=base):
-            for half in range(2):
-                high, low = split(source[n, :, (1 - half) * GW : (2 - half) * GW])
-                p_split[base + n, 0:B, half * GW : (half + 1) * GW] = high
-                p_split[base + n, B : 2 * B, half * GW : (half + 1) * GW] = low
-            return carry
-
-        lax.fori_loop(0, H, split_halo, 0)
+    def take_halo(arriving, source, base):
+        for copy in arriving:
+            copy.wait_recv()
+
+        def split_halo(n, carry):
+            for side in range(2):
+                high, rest = split(source[n, :, (1 - side) * GW : (2 - side) * GW])
+                p_split[base + n, 0:B, side * GW : (side + 1) * GW] = high
+                p_split[base + n, B : 2 * B, side * GW : (side + 1) * GW] = rest
+            return carry
+
+        lax.fori_loop(0, H, split_halo, 0, unroll=2)
 
     near = {}
 
@@ -296,13 +305,21 @@
                 out.at[g], landing[g], near_send.at[side, g], near_recv.at[side, g], where
             )
 
+    take_halo(halo_from_ahead, p_high, R + H)
     rim((R - H) // ROWS, 0, above_out, lower, (0, 1, 2), ahead)
+    take_halo(halo_from_behind, p_low, 0)
     rim(0, 1, below_out, upper, (2, 1, 0), behind)
 
     def sum_own():
         for index in range(2):
             add_own((R - H) // ROWS + index, index)
             add_own(index, 2 + index)
+
+        def inner_own(chunk, carry):
+            add_own(chunk, chunk + 2)
+            return carry
+
+        lax.fori_loop(H // ROWS, (R - H) // ROWS, inner_own, 0)
 
     def build(target, piece):
         a = functools.reduce(jnp.maximum, [here(target, i) * i for i in range(1, G)])
@@ -382,7 +399,7 @@
 
 
 def coarse_rows(columns, aggregate, owner, a_blocks, tentative, slots):
-    anywhere = pl.BlockSpec(memory_space=pl.ANY)
+    hbm = pl.BlockSpec(memory_space=pltpu.HBM)
     vmem = pl.BlockSpec(memory_space=pltpu.VMEM)
     smem = pl.BlockSpec(memory_space=pltpu.SMEM)
     dma = pltpu.SemaphoreType.DMA
@@ -393,7 +410,7 @@
     return pl.pallas_call(
         functools.partial(coarse_kernel, slots),
         out_shape=jax.ShapeDtypeStruct((5 * G, G, BB), f32),
-        in_specs=[smem, smem, smem, anywhere, anywhere],
+        in_specs=[smem, smem, smem, hbm, hbm],
         out_specs=vmem,
         scratch_shapes=[
             pltpu.VMEM((R // 8, K, B // 2 + 1, 8, LANES), f32),
@@ -409,7 +426,7 @@
             pltpu.VMEM((H, B, 2 * GW), f32),
             pltpu.VMEM((H, B, 2 * GW), f32),
             pltpu.VMEM((R + 2 * H, 2 * B, 2 * GW), bf16),
-            pltpu.VMEM((4, 2, CHUNK, 3 * GW), bf16),
+            pltpu.VMEM((R // ROWS, 2, CHUNK, 3 * GW), bf16),
             part, part, part,
             piece, piece, piece, piece, piece, piece,
             pltpu.VMEM((2, H, 8, LANES), jnp.int32),
@@ -420,13 +437,13 @@
             pltpu.VMEM((4 * G * B, LANES), f32),
             dma((1 + R // 8,)),
             dma((4,)), dma((4,)),
-            dma((2,)), dma((2,)),
+            dma((2, 2)), dma((2, 2)),
             dma((2, 3)), dma((2, 3)),
             dma((slots,)), dma((slots,)),
             dma((PIECES, slots)), dma((PIECES, slots)),
         ],
         compiler_params=pltpu.CompilerParams(
-            collective_id=0, has_side_effects=True, vmem_limit_bytes=48 << 20
+            collective_id=0, has_side_effects=True, vmem_limit_bytes=62 << 20
         ),
         name="coarse",
     )(columns.T, aggregate, owner, a_tiled, t_tiled)

time: 86.4 us -> 75 us (0.87)
  Pallas kernels: 79.7 us -> 71.1 us
  local copies, waits for them, and re-layouts: 5.98 us -> 2.5 us
    pallas_call x1, Pallas kernels: 79.7 us -> 71.1 us  [coarse_rows(): pl.pallas_call(functools.partial(coarse_kernel, slots), out_shape=jax.Sha...]
    unnamed x11 -> x1, local copies, waits for them, and re-layouts: 5.98 us -> 2.5 us
where the time goes in v5:
time: 75 us; the launch traced here: 73.6 us
  Pallas kernels  71.1 us (95%)
  local copies, waits for them, and re-layouts  2.5 us (3%)
    pallas_call x1, Pallas kernels, coarse_rows(): pl.pallas_call(functools.partial(coarse_kernel, slots), out_shape=jax.Sha...  71.1 us
    unnamed x1, local copies, waits for them, and re-layouts  2.5 us

profile of v5, /device:TPU:1, one launch (start us, length us, event | category | flops | bytes accessed | tf_op | source)
XLA Modules:
  0.0 73.6 jit_solution(9739317502752204281)
XLA Ops:
  0.0 71.1 %coarse.1 = f32[20,4,4096]{2,1,0:T(4,128)} custom-call(s32[6,32]{1,0:T(8,128)} %bitcast.11, s32[32]{0:T(128)} %aggregate.1, s32[4]{0:T(128)} %owner.1, f32[6,4,32,8,128]{4,3,2,1,0:T(8,128)} %bitcast.9, f32[4,32,8,128]{3,2,1,0:T(8,128)} %bitcast.10), custom_call_target="tpu_custom_call" | custom-call | tf_op jit(solution)/shard_map/coarse/pallas_call | solution.py:410
  71.1 2.5 %copy.7 = f32[4,20,4096]{2,0,1:T(4,128)} copy(f32[4,20,4096]{2,0,1:T(4,128)} %bitcast.8) | data formatting | bytes 2621440
